TPU v7x, 512 devices: a whole 4x4x16 slice. The times are simulated.
512 devices in a mesh: ctx: 64 (over y, z), tp: 8 (over x, core).
Axes of the slice: x: 4, y: 4, z: 16, core: 2. Of those that a mesh axis runs over, the one named last changes fastest.
Arguments:
- queries: bfloat16 [8192, 4096], P('ctx', 'tp'), may hold values from -16 to 16
- keys: bfloat16 [8192, 1024], P('ctx', 'tp'), may hold values from -7.1 to 7.1
- values: bfloat16 [8192, 1024], P('ctx', 'tp'), may hold values from -6 to 6
- mixer_input: bfloat16 [8192, 8192], P('ctx', 'tp'), may hold values from -6 to 6
- gate: bfloat16 [8192, 8192], P('ctx', 'tp'), may hold values from -6 to 6
- step_weight: bfloat16 [8192, 128], P('tp'), may hold values from -0.0625 to 0.0625
- state_weight: bfloat16 [8192, 32], P('tp'), may hold values from -0.0625 to 0.0625
- step_bias: float32 [128], P('tp'), may hold values from -1 to 1
- decay_rate: float32 [128], P('tp'), may hold values from 1.2207031e-06 to 0.05
- skip_gain: float32 [128], P('tp'), may hold values from 0.5 to 2
- norm_gain: float32 [8192], P('tp'), may hold values from 0.1 to 1.9
Outputs:
- attention_out: bfloat16 [8192, 4096], P('ctx', 'tp')
- mamba_out: bfloat16 [8192, 8192], P('ctx', 'tp')
All inputs are finite; a program needn't handle non-finite values.
Results may differ from a plain program's by a relative error of at most 0.0044.
Values may be sent and summed in bfloat16 or wider, within the bound.
A program may use at most 64 MiB of HBM per device.

v0:
```python
import math

import jax
import jax.numpy as jnp
from jax import lax
from jax.sharding import PartitionSpec as P

HD = 128
DECAY_CHANNELS = 64
SCAN_TOKENS = 128


def carried_in(value, axis, join, neutral):
    count, mine = (lax.axis_size(axis), lax.axis_index(axis))
    pieces = jax.tree.map(lambda part: lax.all_gather(part, axis), value)
    subtotal = jax.tree.map(
        lambda part, zero: jnp.full_like(part, 0) + jnp.asarray(zero, part.dtype), value, neutral
    )

    def hop(position, subtotal):
        longer = join(subtotal, jax.tree.map(lambda part: part[position], pieces))
        return jax.tree.map(lambda new, old: jnp.where(position < mine, new, old), longer, subtotal)

    return lax.fori_loop(0, count - 1, hop, subtotal)


def keep_state(previous):
    return previous


def update(previous, query_set, positions, keys_here, values_here, key_positions, scale):
    top, total, summed = previous
    scores = (
        jnp.einsum("tkgd,skd->kgts", query_set, keys_here, preferred_element_type=jnp.float32)
        * scale
    )
    mask = key_positions[None, :] <= positions[:, None]
    scores = jnp.where(mask, scores, -1e30)
    new_top = jnp.maximum(top, jnp.max(scores, axis=-1))
    weights = jnp.where(mask, jnp.exp(scores - new_top[..., None]), 0.0)
    new_total = jnp.sum(weights, axis=-1)
    product = jnp.einsum(
        "kgts,skd->kgtd",
        weights.astype(jnp.bfloat16),
        values_here,
        preferred_element_type=jnp.float32,
    )
    return (new_top, new_total, product)


def finish(state, length):
    top, total, summed = state
    result = summed / total[..., None]
    result = jnp.transpose(result, (2, 0, 1, 3))
    return result.reshape(length, -1).astype(jnp.bfloat16)


def attention_layer(queries, keys, values):
    length = queries.shape[0]
    kv_heads = keys.shape[1] // HD
    group = queries.shape[1] // keys.shape[1]
    scale = 1.0 / math.sqrt(HD)
    own_index = lax.axis_index("ctx")
    sets = [(queries, own_index * length + jnp.arange(length, dtype=jnp.int32))]
    shaped = [
        (query_set.reshape(query_set.shape[0], kv_heads, group, HD), positions)
        for query_set, positions in sets
    ]
    initial = tuple(
        (
            (
                jnp.full((kv_heads, group, positions.shape[0]), -1e30, jnp.float32),
                jnp.zeros((kv_heads, group, positions.shape[0]), jnp.float32),
                jnp.zeros((kv_heads, group, positions.shape[0], HD), jnp.float32),
            )
            for query_set, positions in shaped
        )
    )

    def fold(carry, pieces, start_index):
        key_piece, value_piece = pieces
        rows = key_piece.shape[0]
        keys_here = key_piece.reshape(rows, kv_heads, HD)
        values_here = value_piece.reshape(rows, kv_heads, HD)
        key_positions = jnp.arange(rows, dtype=jnp.int32)
        result = []
        for (query_set, positions), state in zip(shaped, carry):

            def compute(previous, query_set=query_set, positions=positions):
                return update(
                    previous, query_set, positions, keys_here, values_here, key_positions, scale
                )

            result.append(lax.cond(start_index > positions[-1], keep_state, compute, state))
        return tuple(result)

    final = fold(
        initial,
        (
            lax.all_gather(keys, "ctx", axis=0, tiled=True),
            lax.all_gather(values, "ctx", axis=0, tiled=True),
        ),
        jnp.int32(0),
    )
    outputs = [
        finish(state, query_set.shape[0]) for state, (query_set, positions) in zip(final, shaped)
    ]
    return outputs[0]


def mixer_layer(
    mixer_input, gate, step_weight, state_weight, step_bias, decay_rate, skip_gain, norm_gain
):
    length, channel_count = mixer_input.shape
    head_count = channel_count // DECAY_CHANNELS
    state_length = state_weight.shape[1] // 2
    part_step = jnp.dot(mixer_input, step_weight, preferred_element_type=jnp.float32)
    part_maps = jnp.dot(mixer_input, state_weight, preferred_element_type=jnp.float32)
    summed, maps = lax.psum((part_step, part_maps), "tp")
    step_raw = lax.dynamic_slice_in_dim(summed, lax.axis_index("tp") * head_count, head_count, 1)
    step = jax.nn.softplus(step_raw + step_bias)
    log_decay = -decay_rate * step
    block_count = length // SCAN_TOKENS
    decay_blocks = log_decay.reshape(block_count, SCAN_TOKENS, head_count)
    step_blocks = step.reshape(block_count, SCAN_TOKENS, head_count)
    b_rows = maps[:, :state_length].reshape(block_count, SCAN_TOKENS, state_length)
    c_rows = maps[:, state_length:].reshape(block_count, SCAN_TOKENS, state_length)
    input_blocks = mixer_input.reshape(block_count, SCAN_TOKENS, head_count, DECAY_CHANNELS)
    climb = jnp.cumsum(decay_blocks, axis=1)
    inner = jnp.einsum("ctn,csn->cts", c_rows, b_rows, precision=lax.Precision.HIGHEST)
    causal = (jnp.arange(SCAN_TOKENS)[:, None] >= jnp.arange(SCAN_TOKENS)[None, :])[None, None]
    climb_t = jnp.swapaxes(climb, 1, 2)
    diff = climb_t[:, :, :, None] - climb_t[:, :, None, :]
    decay = jnp.where(causal, jnp.exp(jnp.where(causal, diff, 0.0)), 0.0)
    mix = (inner[:, None] * decay * jnp.swapaxes(step_blocks, 1, 2)[:, :, None, :]).astype(
        jnp.bfloat16
    )
    local = jnp.einsum("chts,cshp->cthp", mix, input_blocks, preferred_element_type=jnp.float32)
    final = climb[:, -1, :]
    feed = (
        b_rows[:, :, :, None] * (jnp.exp(final[:, None, :] - climb) * step_blocks)[:, :, None, :]
    ).astype(jnp.bfloat16)
    contrib = jnp.einsum("csnh,cshp->cnhp", feed, input_blocks, preferred_element_type=jnp.float32)
    running_state = jnp.zeros((state_length, head_count, DECAY_CHANNELS), jnp.float32)
    before = jnp.zeros((head_count,), jnp.float32)
    entering = running_state
    befores = before
    running_state = jnp.exp(final[0])[None, :, None] * running_state + contrib[0]
    before = final[0]
    state_flattened = running_state.reshape(state_length, head_count * DECAY_CHANNELS)

    def combine(earlier, later_blocks):
        decay_factor = jnp.repeat(jnp.exp(later_blocks[0]), DECAY_CHANNELS)
        return (earlier[0] + later_blocks[0], decay_factor[None, :] * earlier[1] + later_blocks[1])

    empty = (jnp.zeros_like(before), jnp.zeros_like(state_flattened))
    incoming_state = carried_in((before, state_flattened), "ctx", combine, empty)[1]
    incoming_state = incoming_state.reshape(state_length, head_count, DECAY_CHANNELS)
    starts = jnp.stack([entering + jnp.exp(befores)[None, :, None] * incoming_state])
    carried = jnp.exp(climb)[..., None] * jnp.einsum(
        "ctn,cnhp->cthp", c_rows, starts, precision=lax.Precision.HIGHEST
    )
    y_blocks = local + carried + skip_gain[None, None, :, None] * input_blocks.astype(jnp.float32)
    y_flat = y_blocks.reshape(length, channel_count)
    gated = y_flat * jax.nn.silu(gate.astype(jnp.float32))
    square_sum = lax.psum(jnp.sum(gated * gated, axis=-1, keepdims=True), "tp")
    mean_square = square_sum / (channel_count * lax.axis_size("tp"))
    return (gated * lax.rsqrt(mean_square + 1e-05) * norm_gain).astype(jnp.bfloat16)


def per_device(
    queries,
    keys,
    values,
    mixer_input,
    gate,
    step_weight,
    state_weight,
    step_bias,
    decay_rate,
    skip_gain,
    norm_gain,
):
    attention_out = attention_layer(queries, keys, values)
    mamba_out = mixer_layer(
        mixer_input, gate, step_weight, state_weight, step_bias, decay_rate, skip_gain, norm_gain
    )
    return (attention_out, mamba_out)


def solution(mesh):
    return jax.shard_map(
        per_device,
        mesh=mesh,
        in_specs=(
            P("ctx", "tp"),
            P("ctx", "tp"),
            P("ctx", "tp"),
            P("ctx", "tp"),
            P("ctx", "tp"),
            P("tp", None),
            P("tp", None),
            P("tp"),
            P("tp"),
            P("tp"),
            P("tp"),
        ),
        out_specs=(P("ctx", "tp"), P("ctx", "tp")),
        check_vma=False,
    )
```

profile of v0, /device:TPU:1, one launch (start us, length us, event | category | flops | bytes accessed | tf_op | source)
XLA Modules:
  0.0 534.9 jit_solution(488199834054100313)
XLA Ops:
  8.1 0.9 copy-done
  9.0 1.9 fusion.48
  12.1 1.1 copy.44
  13.8 1.1 fusion.47
  15.0 26.9 %psum.21 = f32[128,32]{0,1:T(8,128)S(1)} all-reduce(f32[128,32]{0,1:T(8,128)S(1)} %fusion.47), channel_id=1, replica_groups=mesh['ctx'=64,'tp'=8] {'tp'}, use_global_device_ids=true, to_apply=%region_4.5 | all-reduce | flops 4096 | bytes 32768 | tf_op jit(solution)/shard_map/psum | solution.py:119
  41.8 49.6 %all-reduce.2.cloned.1.call-done = f32[128,128]{0,1:T(8,128)} async-done(((f32[128,128]{0,1:T(8,128)}), f32[128,128]{0,1:T(8,128)}) %all-reduce.2.cloned.1.call-update) | async-done | bytes 65552 | tf_op jit(solution)/shard_map/psum | solution.py:119
  94.6 1.1 copy.48
  97.3 67.5 %all-gather = f32[64,1,16]{2,1,0:T(1,128)S(1)} all-gather(f32[1,1,16]{2,1,0:T(1,128)S(1)} %get-tuple-element.154), channel_id=2, replica_groups=mesh['ctx'=64,'tp'=8] {'ctx'}, dimensions={0}, use_global_device_ids=true | all-gather | bytes 4160 | tf_op jit(solution)/shard_map/all_gather | solution.py:15
  164.8 126.1 %all-gather.7.cloned.1.call-done = bf16[8192,128]{1,0:T(8,128)(2,1)} async-done(((bf16[128,128]{1,0:T(8,128)(2,1)}), bf16[8192,128]{1,0:T(8,128)(2,1)}) %all-gather.7.cloned.1.call-update) | async-done | bytes 2097168 | tf_op jit(solution)/shard_map/all_gather | solution.py:101
  290.9 16.8 %conditional.1 = (f32[1,4,128]{2,1,0:T(4,128)S(1)}, f32[1,4,128,128]{3,2,1,0:T(8,128)S(1)}) conditional(s32[]{:T(128)} %bitcast.7, (s32[8192]{0:T(1024)S(1)}, s32[128]{0:T(128)S(1)}, bf16[128,512]{1,0:T(8,128)(2,1)}, bf16[8192,128]{1,0:T(8,128)(2,1)}, bf16[8192,128]{1,0:T(8,128)(2,1)}) %tuple.30, () %tuple.31), branch_computations={%region_0.3_spmd, %region_3.4_spmd} | conditional | flops 2203057664 | bytes 67547696 | solution.py:94
  290.9 3.7 broadcast_compare_fusion
  294.7 3.9 fusion
  298.6 4.2 fusion.2
  302.8 4.8 fusion.10
  308.7 127.7 %all-gather.9.cloned.1.call-done = f32[64,16,1024]{2,1,0:T(8,128)} async-done(((f32[1,16,1024]{2,1,0:T(8,128)}), f32[64,16,1024]{2,1,0:T(8,128)}) %all-gather.9.cloned.1.call-update) | async-done | bytes 4194320 | tf_op jit(solution)/shard_map/all_gather | solution.py:15
  436.4 66.2 %while.14 = (s32[]{:T(128)}, f32[16,1024]{1,0:T(8,128)S(1)}, s32[]{:T(128)}, f32[64,16]{1,0:T(8,128)S(1)}, f32[64,16,1024]{2,1,0:T(8,128)}, /*index=5*/s32[]{:T(128)}, s32[]{:T(128)}) while((s32[]{:T(128)}, f32[16,1024]{1,0:T(8,128)S(1)}, s32[]{:T(128)}, f32[64,16]{1,0:T(8,128)S(1)}, f32[64,16,1024]{2,1,0:T(8,128)}, ...), condition=%wide.region_8.9_spmd.clone, body=%wide.region_7.8_spmd.clone.sunk | while | flops 65540 | bytes 213297 | solution.py:24
  436.6 0.9 fusion.57
  437.6 0.9 fusion.57
  438.7 0.9 fusion.57
  439.7 0.9 fusion.57
  440.8 0.9 fusion.57
  441.8 0.9 fusion.57
  442.9 0.9 fusion.57
  443.9 0.9 fusion.57
  445.0 0.9 fusion.57
  446.0 0.9 fusion.57
  447.1 0.9 fusion.57
  448.1 0.9 fusion.57
  449.2 0.9 fusion.57
  450.2 0.9 fusion.57
  451.3 0.9 fusion.57
  452.3 0.9 fusion.57
  455.5 0.9 fusion.57
  458.6 0.9 fusion.57
  461.8 0.9 fusion.57
  464.9 0.9 fusion.57
  472.3 0.9 fusion.57
  475.4 0.9 fusion.57
  478.6 0.9 fusion.57
  481.7 0.9 fusion.57
  484.9 0.9 fusion.57
  492.2 0.9 fusion.57
  495.4 0.9 fusion.57
  498.5 0.9 fusion.57
  501.7 0.9 fusion.57
  502.7 1.0 fusion.21
  504.7 21.6 %psum.23 = f32[128,1]{0,1:T(1,128)S(1)} all-reduce(f32[128,1]{0,1:T(1,128)S(1)} %bitcast.131), channel_id=1, replica_groups=mesh['ctx'=64,'tp'=8] {'tp'}, use_global_device_ids=true, to_apply=%region_10.11 | all-reduce | flops 128 | bytes 1024 | tf_op jit(solution)/shard_map/psum | solution.py:166
  526.4 0.9 multiply_convert_fusion.2
  (272 shorter events, 47.4 us)
Async XLA Ops:
  8.0 1.0 copy-start
  8.0 83.4 %all-reduce.2.cloned.1.call-start = ((), (), s32[]{:S(2)}) async-start(), calls=%async_computation.2 | async-start | bytes 131072 | tf_op jit(solution)/shard_map/psum | solution.py:119
  10.8 154.0 %all-gather.5.cloned.1.call-start = ((), (), s32[]{:S(2)}) async-start(), calls=%async_computation | async-start | bytes 2129920 | tf_op jit(solution)/shard_map/all_gather | solution.py:100
  11.4 279.5 %all-gather.7.cloned.1.call-start = ((), (), s32[]{:S(2)}) async-start(), calls=%async_computation.1 | async-start | bytes 2129920 | tf_op jit(solution)/shard_map/all_gather | solution.py:101
  12.0 424.4 %all-gather.9.cloned.1.call-start = ((), (), s32[]{:S(2)}) async-start(), calls=%async_computation.3 | async-start | bytes 4259840 | tf_op jit(solution)/shard_map/all_gather | solution.py:15
  290.9 212.8 %copy-start.4 = (f32[16]{0:T(128)S(1)}, f32[16]{0:T(128)}, u32[]{:S(2)}) copy-start(f32[16]{0:T(128)} %param.24) | copy-start | bytes 196
  290.9 213.6 %copy-start.1 = (bf16[128,1024]{1,0:T(8,128)(2,1)S(1)}, bf16[128,1024]{1,0:T(8,128)(2,1)}, u32[]{:S(2)}) copy-start(bf16[128,1024]{1,0:T(8,128)(2,1)} %param.19) | copy-start | bytes 786436
  290.9 235.5 %copy-start.2 = (f32[1024]{0:T(1024)S(1)}, f32[1024]{0:T(1024)}, u32[]{:S(2)}) copy-start(f32[1024]{0:T(1024)} %param.25) | copy-start | bytes 12292
  294.7 8.1 %copy-start.3 = (bf16[8192,128]{1,0:T(8,128)(2,1)S(1)}, bf16[8192,128]{1,0:T(8,128)(2,1)}, u32[]{:S(2)}) copy-start(bf16[8192,128]{1,0:T(8,128)(2,1)} %get-tuple-element.104) | copy-start | bytes 6291460 | tf_op jit(solution)/shard_map/cond
Sparse Core Ops, SparseCore 0:
  11.7 79.6 all-reduce.1
Sparse Core Ops, SparseCore 1:
  14.3 136.9 all-gather.4
  154.0 136.8 all-gather.6
  294.3 142.0 all-gather.8
where the time goes:
time: 538 us; the launch traced here: 535 us
  waiting for transfers between devices  304 us (57%)
  blocking collectives  116 us (22%)
  other arithmetic  67.2 us (12%)
  between operations  16.5 us (3%)
  local copies, waits for them, and re-layouts  15 us (3%)
  matrix products  13.8 us (3%)
    all_gather x1, waiting for transfers between devices, carried_in(): pieces = jax.tree.map(lambda part: lax.all_gather(part, axis), value)  128 us
    all_gather x1, waiting for transfers between devices, attention_layer(): lax.all_gather(values, 'ctx', axis=0, tiled=True)  126 us
    all_gather x1, blocking collectives, carried_in(): pieces = jax.tree.map(lambda part: lax.all_gather(part, axis), value)  67.5 us
    select_n x63, other arithmetic, hop(): jnp.where(position < mine, new, old)  54.9 us
    psum x1, waiting for transfers between devices, mixer_layer(): summed, maps = lax.psum((part_step, part_maps), 'tp')  49.6 us
    psum x1, blocking collectives, mixer_layer(): summed, maps = lax.psum((part_step, part_maps), 'tp')  26.9 us
    psum x1, blocking collectives, mixer_layer(): square_sum = lax.psum(jnp.sum(gated * gated, axis=-1, keepdims=True), 'tp')  21.6 us
  transfers between devices with their start and end apart: 4, of which 3 were waited for; matrix products, arithmetic and copies ran while one was open for 5% of the time, Pallas kernels for 0%

commit v1 on v0

v1 whole, which is shorter than its diff:
```python
import functools
import math

import jax
import jax.numpy as jnp
from jax import lax
from jax.experimental import pallas as pl
from jax.experimental.pallas import tpu as pltpu
from jax.sharding import PartitionSpec as P

HD = 128
TOK = 128
ROW = 16
ROWS = 4
TP = 8
HEADS = 16
STATE = 16
PAIRS = 8
CHANNELS = 8192
SCALE = 1.0 / math.sqrt(HD)
F32 = jnp.float32
BF16 = jnp.bfloat16
EXACT = lax.Precision.HIGHEST
MESH = pl.DeviceIdType.MESH


def dot(a, b, precision=None):
    return jnp.dot(a, b, preferred_element_type=F32, precision=precision)


def dot_t(a, b, precision=None):
    return lax.dot_general(
        a, b, (((1,), (1,)), ((), ())), preferred_element_type=F32, precision=precision
    )


def kernel(
    q_ref, k_ref, v_ref, x_ref, gate_ref, ws_ref, wm_ref, bias_ref, rate_ref, skip_ref, norm_ref,
    attn_ref, mamba_ref,
    kbuf, vbuf, qbuf, obuf, orecv, stat_send, stat_recv, own_out, acc_out,
    proj_send, proj_recv, csend, crecv, fsend, frecv, ysend, yrecv, rsend, srecv,
    base, gated, sqsend, sqrecv, pref,
    ring_ss, ring_rs, q_ss, q_rs, o_ss, o_rs, st_ss, st_rs, grp_ss, grp_rs,
):
    me = lax.axis_index("ctx")
    t = lax.axis_index("tp")
    y, z = me // ROW, me % ROW

    def tp_peer(o):
        return lax.rem(t + o, TP)

    def z_peer(o):
        return y * ROW + lax.rem(z + o + ROW, ROW)

    def y_peer(o):
        return lax.rem(y + o + ROWS, ROWS) * ROW + z

    def at(ctx, tp):
        return {"ctx": ctx, "tp": tp}

    barrier = pltpu.get_barrier_semaphore()
    for o in range(1, TP):
        pl.semaphore_signal(barrier, inc=1, device_id=at(me, tp_peer(o)), device_id_type=MESH)
    for o in range(1, ROW):
        pl.semaphore_signal(barrier, inc=1, device_id=at(z_peer(o), t), device_id_type=MESH)
    for o in range(1, ROWS):
        pl.semaphore_signal(barrier, inc=1, device_id=at(y_peer(o), t), device_id_type=MESH)

    ws = dot(x_ref[...], ws_ref[...])
    wm = dot(x_ref[...], wm_ref[...])
    step_part = ws.T
    maps_part = jnp.concatenate([wm, jnp.zeros((TOK, 96), F32)], axis=1).T[:32]
    for p in range(TP):
        proj_send[p, 0:16, :] = step_part[16 * p:16 * p + 16]
        proj_send[p, 16:48, :] = maps_part
    kbuf[z] = k_ref[...]
    vbuf[z] = v_ref[...]

    pl.semaphore_wait(barrier, TP - 1 + ROW - 1 + ROWS - 1)

    def remote(src, dst, ssem, rsem, ctx, tp):
        return pltpu.make_async_remote_copy(
            src_ref=src, dst_ref=dst, send_sem=ssem, recv_sem=rsem,
            device_id=at(ctx, tp), device_id_type=MESH,
        )

    def proj_copy(o):
        return remote(
            proj_send.at[tp_peer(o)], proj_recv.at[t], grp_ss.at[0], grp_rs.at[0], me, tp_peer(o)
        )

    for o in range(1, TP):
        proj_copy(o).start()

    def ring_copy(kv, d, s):
        block = lax.rem(z - d * (s - 1) + 2 * ROW, ROW)
        buf = (kbuf, vbuf)[kv]
        i = 0 if d > 0 else 1
        src = (k_ref, v_ref)[kv] if s == 1 else buf.at[block]
        return remote(
            src, buf.at[block], ring_ss.at[kv, i, s - 1], ring_rs.at[kv, i, s - 1], z_peer(d), t
        )

    def ring_steps(d):
        return ROW // 2 if d > 0 else ROW // 2 - 1

    for kv in (0, 1):
        for d in (1, -1):
            ring_copy(kv, d, 1).start()

    def ring(s):
        for kv in (0, 1):
            for d in (1, -1):
                if s <= ring_steps(d):
                    ring_copy(kv, d, s).wait_recv()
                    if s + 1 <= ring_steps(d):
                        ring_copy(kv, d, s + 1).start()

    def q_copy(o):
        return remote(q_ref, qbuf.at[o - 1], q_ss.at[o - 1], q_rs.at[o - 1], y_peer(-o), t)

    for o in range(1, ROWS):
        @pl.when(y >= o)
        def _(o=o):
            q_copy(o).start()

    lane = lax.broadcasted_iota(jnp.int32, (TOK, TOK), 1)
    sub = lax.broadcasted_iota(jnp.int32, (TOK, TOK), 0)
    low = lane < 64
    sub16 = lax.broadcasted_iota(jnp.int32, (HEADS, TOK), 0)
    lane16 = lax.broadcasted_iota(jnp.int32, (HEADS, TOK), 1)

    def column(ref):
        out = jnp.full((HEADS, TOK), ref[0], F32)
        for h in range(1, HEADS):
            out = jnp.where(sub16 == h, ref[h], out)
        return out

    bias, rate = column(bias_ref), column(rate_ref)
    ring(1)

    remote(
        proj_send.at[0:TP - 1], proj_recv.at[0:TP - 1], grp_ss.at[0], grp_rs.at[0], me, tp_peer(1)
    ).wait_recv()
    proj_recv[t] = proj_send[t]
    total = proj_recv[0]
    for p in range(1, TP):
        total = total + proj_recv[p]
    b_rows, c_rows = total[16:32], total[32:48]
    raw = total[0:16] + bias
    step = jnp.maximum(raw, 0.0) + jnp.log1p(jnp.exp(-jnp.abs(raw)))
    climb = -rate * step
    for sh in (1, 2, 4, 8, 16, 32, 64):
        climb = climb + jnp.where(lane16 >= sh, pltpu.roll(climb, sh, axis=1), 0.0)
    final = jnp.broadcast_to(climb[:, TOK - 1:TOK], (HEADS, TOK))
    for j in range(PAIRS):
        fsend[j] = jnp.where(low[0:1], final[2 * j:2 * j + 1], final[2 * j + 1:2 * j + 2])
    def f_copy(o):
        return remote(
            fsend.at[lax.rem(z + o, ROW) // 2], frecv.at[z], grp_ss.at[1], grp_rs.at[1],
            z_peer(o), t,
        )

    for o in range(1, ROW):
        f_copy(o).start()
    feed_weight = jnp.exp(final - climb) * step

    def pair_input(j):
        xp = x_ref[:, 128 * j:128 * j + 128]
        zero = jnp.zeros_like(xp)
        return jnp.concatenate([jnp.where(low, xp, zero), jnp.where(low, zero, xp)], axis=0)

    for j in range(PAIRS):
        feed = jnp.concatenate(
            [b_rows * feed_weight[h:h + 1] for h in (2 * j, 2 * j + 1)], axis=1
        ).astype(BF16)
        contrib = dot(feed, pair_input(j))
        csend[2 * j] = contrib[0:8]
        csend[2 * j + 1] = contrib[8:16]

    def c_copy(o):
        return remote(
            csend.at[lax.rem(z + o, ROW)], crecv.at[z], grp_ss.at[2], grp_rs.at[2], z_peer(o), t
        )

    for o in range(1, ROW):
        c_copy(o).start()
    crecv[z] = csend[z]
    frecv[z] = fsend[z // 2]
    ring(2)

    turned = jnp.concatenate([c_rows, climb, jnp.exp(climb), jnp.zeros((80, TOK), F32)], axis=0).T
    c_cols = turned[:, 0:16]
    inner = dot(c_cols, b_rows, EXACT)
    causal = sub >= lane

    def local_pair(j):
        mixes = []
        for h in (2 * j, 2 * j + 1):
            diff = turned[:, 16 + h:17 + h] - climb[h:h + 1]
            mix = inner * jnp.exp(diff) * step[h:h + 1]
            mixes.append(jnp.where(causal, mix, 0.0).astype(BF16))
        out = dot(jnp.concatenate(mixes, axis=1), pair_input(j))
        gain = jnp.where(low, skip_ref[2 * j], skip_ref[2 * j + 1])
        cols = slice(128 * j, 128 * j + 128)
        base[:, cols] = out + gain * x_ref[:, cols].astype(F32)

    for j in range(4):
        local_pair(j)
    ring(3)
    for j in range(4, PAIRS):
        local_pair(j)
    ring(4)
    ring(5)

    remote(
        csend.at[0:ROW - 1], crecv.at[0:ROW - 1], grp_ss.at[2], grp_rs.at[2], z_peer(1), t
    ).wait_recv()
    remote(
        frecv.at[0:ROW - 1], frecv.at[0:ROW - 1], grp_ss.at[1], grp_rs.at[1], z_peer(1), t
    ).wait_recv()
    running = jnp.zeros((8, TOK), F32)
    passed = jnp.zeros((1, TOK), F32)
    gone = []
    for b in range(ROW):
        pref[b] = running
        gone.append(passed)
        running = jnp.exp(frecv[b]) * running + crecv[b]
        passed = passed + frecv[b]
    ysend[0:8] = running
    ysend[8:16] = jnp.broadcast_to(passed, (8, TOK))

    def y_copy(o):
        return remote(ysend, yrecv.at[y], grp_ss.at[3], grp_rs.at[3], y_peer(o), t)

    for o in range(1, ROWS):
        y_copy(o).start()
    yrecv[y] = ysend[...]
    ring(6)
    remote(
        yrecv.at[0:ROWS - 1], yrecv.at[0:ROWS - 1], grp_ss.at[3], grp_rs.at[3], y_peer(1), t
    ).wait_recv()
    enter = jnp.zeros((8, TOK), F32)
    for r in range(ROWS - 1):
        longer = jnp.exp(yrecv[r, 8:16]) * enter + yrecv[r, 0:8]
        enter = jnp.where(r < y, longer, enter)
    for b in range(ROW):
        rsend[b] = pref[b] + jnp.exp(gone[b]) * enter

    def r_copy(o):
        return remote(
            rsend.at[lax.rem(z + o, ROW)], srecv.at[z], grp_ss.at[4], grp_rs.at[4], z_peer(o), t
        )

    for o in range(1, ROW):
        r_copy(o).start()
    srecv[z] = rsend[z]
    ring(7)
    ring(8)

    keys = ROW * TOK

    def unit(q, masked):
        scores = dot_t(q, kbuf[...].reshape(keys, HD)) * SCALE
        if masked:
            key = lax.broadcasted_iota(jnp.int32, (TOK, keys), 1)
            query = lax.broadcasted_iota(jnp.int32, (TOK, keys), 0) + z * TOK
            mask = key <= query
            scores = jnp.where(mask, scores, -1e30)
        top = jnp.max(scores, axis=1, keepdims=True)
        weights = jnp.exp(scores - top)
        if masked:
            weights = jnp.where(mask, weights, 0.0)
        whole = jnp.sum(weights, axis=1, keepdims=True)
        mixed = dot(weights.astype(BF16), vbuf[...].reshape(keys, HD))
        return mixed / whole, top, whole

    def stats_of(tops, wholes):
        out = jnp.zeros((TOK, TOK), F32)
        for i, col in enumerate(tops + wholes):
            out = jnp.where(lane == i, col, out)
        return out

    def o_copy(o, h):
        cols = slice(128 * h, 128 * h + 128)
        return remote(
            obuf.at[o - 1, h], orecv.at[o - 1, h],
            o_ss.at[o - 1, h], o_rs.at[o - 1, h], y_peer(o), t,
        )

    def st_copy(o):
        return remote(
            stat_send.at[o - 1], stat_recv.at[o - 1], st_ss.at[o - 1], st_rs.at[o - 1],
            y_peer(o), t,
        )

    for o in (3, 2, 1):
        @pl.when(y + o < ROWS)
        def _(o=o):
            q_copy(o).wait_recv()
            tops, wholes = [], []
            for h in range(4):
                mixed, top, whole = unit(qbuf[o - 1, :, 128 * h:128 * h + 128], False)
                obuf[o - 1, h] = mixed.astype(BF16)
                o_copy(o, h).start()
                tops.append(top)
                wholes.append(whole)
            stat_send[o - 1] = stats_of(tops, wholes).T[0:8]
            st_copy(o).start()

    tops, wholes = [], []
    for h in range(4):
        mixed, top, whole = unit(q_ref[:, 128 * h:128 * h + 128], True)
        acc_out[:, 128 * h:128 * h + 128] = mixed
        tops.append(top)
        wholes.append(whole)
    own_out[...] = stats_of(tops, wholes)

    remote(
        rsend.at[0:ROW - 1], srecv.at[0:ROW - 1], grp_ss.at[4], grp_rs.at[4], z_peer(1), t
    ).wait_recv()
    squares = jnp.zeros((TOK, TOK), F32)
    for j in range(PAIRS):
        cols = slice(128 * j, 128 * j + 128)
        state = srecv[2 * j:2 * j + 2].reshape(STATE, TOK)
        grown = jnp.where(low, turned[:, 32 + 2 * j:33 + 2 * j], turned[:, 33 + 2 * j:34 + 2 * j])
        out = base[:, cols] + grown * dot(c_cols, state, EXACT)
        g = gate_ref[:, cols].astype(F32)
        out = out * (g / (1.0 + jnp.exp(-g)))
        gated[:, cols] = out
        squares = squares + out * out
    sqsend[...] = dot_t(jnp.ones((8, TOK), F32), squares, EXACT)

    def sq_copy(o):
        return remote(sqsend, sqrecv.at[t], grp_ss.at[5], grp_rs.at[5], me, tp_peer(o))

    for o in range(1, TP):
        sq_copy(o).start()
    sqrecv[t] = sqsend[...]

    for o in range(1, ROWS):
        @pl.when(y >= o)
        def _(o=o):
            st_copy(o).wait_recv()
            other = jnp.concatenate([stat_recv[o - 1], jnp.zeros((120, TOK), F32)], axis=0).T
            mine = own_out[...]
            tops, wholes = [], []
            for h in range(4):
                o_copy(o, h).wait_recv()
                cols = slice(128 * h, 128 * h + 128)
                top_a, top_b = mine[:, h:h + 1], other[:, h:h + 1]
                top = jnp.maximum(top_a, top_b)
                part_a = mine[:, 4 + h:5 + h] * jnp.exp(top_a - top)
                part_b = other[:, 4 + h:5 + h] * jnp.exp(top_b - top)
                whole = part_a + part_b
                acc_out[:, cols] = (
                    acc_out[:, cols] * (part_a / whole)
                    + orecv[o - 1, h].astype(F32) * (part_b / whole)
                )
                tops.append(top)
                wholes.append(whole)
            own_out[...] = stats_of(tops, wholes)

    attn_ref[...] = acc_out[...].astype(BF16)

    remote(
        sqrecv.at[0:TP - 1], sqrecv.at[0:TP - 1], grp_ss.at[5], grp_rs.at[5], me, tp_peer(1)
    ).wait_recv()
    square = sqrecv[0]
    for p in range(1, TP):
        square = square + sqrecv[p]
    inverse = lax.rsqrt(square[0:1] / CHANNELS + 1e-5)
    inverse = jnp.broadcast_to(inverse, (TOK, TOK)).T
    for j in range(PAIRS):
        cols = slice(128 * j, 128 * j + 128)
        mamba_ref[:, cols] = (gated[:, cols] * inverse * norm_ref[0:1, cols]).astype(BF16)

    remote(
        proj_send.at[0:TP - 1], proj_recv.at[0:TP - 1], grp_ss.at[0], grp_rs.at[0], me, tp_peer(1)
    ).wait_send()
    remote(
        frecv.at[0:ROW - 1], frecv.at[0:ROW - 1], grp_ss.at[1], grp_rs.at[1], z_peer(1), t
    ).wait_send()
    remote(
        csend.at[0:ROW - 1], crecv.at[0:ROW - 1], grp_ss.at[2], grp_rs.at[2], z_peer(1), t
    ).wait_send()
    remote(
        yrecv.at[0:ROWS - 1], yrecv.at[0:ROWS - 1], grp_ss.at[3], grp_rs.at[3], y_peer(1), t
    ).wait_send()
    remote(
        rsend.at[0:ROW - 1], srecv.at[0:ROW - 1], grp_ss.at[4], grp_rs.at[4], z_peer(1), t
    ).wait_send()
    remote(
        sqrecv.at[0:TP - 1], sqrecv.at[0:TP - 1], grp_ss.at[5], grp_rs.at[5], me, tp_peer(1)
    ).wait_send()
    for kv in (0, 1):
        for d in (1, -1):
            for s in range(1, ring_steps(d) + 1):
                ring_copy(kv, d, s).wait_send()
    for o in range(1, ROWS):
        @pl.when(y >= o)
        def _(o=o):
            q_copy(o).wait_send()

        @pl.when(y + o < ROWS)
        def _(o=o):
            for h in range(4):
                o_copy(o, h).wait_send()
            st_copy(o).wait_send()


def per_device(
    queries, keys, values, mixer_input, gate, step_weight, state_weight, step_bias, decay_rate,
    skip_gain, norm_gain,
):
    vmem = pl.BlockSpec(memory_space=pltpu.VMEM)
    smem = pl.BlockSpec(memory_space=pltpu.SMEM)
    return pl.pallas_call(
        kernel,
        out_shape=(
            jax.ShapeDtypeStruct((TOK, 4 * HD), BF16),
            jax.ShapeDtypeStruct((TOK, 1024), BF16),
        ),
        in_specs=[vmem] * 7 + [smem] * 3 + [vmem],
        out_specs=(vmem, vmem),
        scratch_shapes=[
            pltpu.VMEM((ROW, TOK, HD), BF16),
            pltpu.VMEM((ROW, TOK, HD), BF16),
            pltpu.VMEM((3, TOK, 4 * HD), BF16),
            pltpu.VMEM((3, 4, TOK, HD), BF16),
            pltpu.VMEM((3, 4, TOK, HD), BF16),
            pltpu.VMEM((3, 8, TOK), F32),
            pltpu.VMEM((3, 8, TOK), F32),
            pltpu.VMEM((TOK, TOK), F32),
            pltpu.VMEM((TOK, 4 * HD), F32),
            pltpu.VMEM((TP, 48, TOK), F32),
            pltpu.VMEM((TP, 48, TOK), F32),
            pltpu.VMEM((ROW, 8, TOK), F32),
            pltpu.VMEM((ROW, 8, TOK), F32),
            pltpu.VMEM((PAIRS, 1, TOK), F32),
            pltpu.VMEM((ROW, 1, TOK), F32),
            pltpu.VMEM((16, TOK), F32),
            pltpu.VMEM((ROWS, 16, TOK), F32),
            pltpu.VMEM((ROW, 8, TOK), F32),
            pltpu.VMEM((ROW, 8, TOK), F32),
            pltpu.VMEM((TOK, 1024), F32),
            pltpu.VMEM((TOK, 1024), F32),
            pltpu.VMEM((8, TOK), F32),
            pltpu.VMEM((TP, 8, TOK), F32),
            pltpu.VMEM((ROW, 8, TOK), F32),
            pltpu.SemaphoreType.DMA((2, 2, 8)),
            pltpu.SemaphoreType.DMA((2, 2, 8)),
            pltpu.SemaphoreType.DMA((3,)),
            pltpu.SemaphoreType.DMA((3,)),
            pltpu.SemaphoreType.DMA((3, 4)),
            pltpu.SemaphoreType.DMA((3, 4)),
            pltpu.SemaphoreType.DMA((3,)),
            pltpu.SemaphoreType.DMA((3,)),
            pltpu.SemaphoreType.DMA((6,)),
            pltpu.SemaphoreType.DMA((6,)),
        ],
        compiler_params=pltpu.CompilerParams(
            collective_id=0, has_side_effects=True, vmem_limit_bytes=48 << 20
        ),
    )(
        queries, keys, values, mixer_input, gate, step_weight, state_weight, step_bias,
        decay_rate, skip_gain, norm_gain.reshape(1, -1),
    )


def solution(mesh):
    return jax.shard_map(
        per_device,
        mesh=mesh,
        in_specs=(P("ctx", "tp"),) * 5 + (P("tp", None),) * 2 + (P("tp"),) * 4,
        out_specs=(P("ctx", "tp"), P("ctx", "tp")),
        check_vma=False,
    )
```

time: 538 us -> 70.5 us (0.13)
  waiting for transfers between devices: 304 us -> 0 us
  blocking collectives: 116 us -> 0 us
  other arithmetic: 67.2 us -> 0 us
  Pallas kernels: 0 us -> 63.6 us
  between operations: 16.5 us -> 0.75 us
  matrix products: 13.8 us -> 0 us
  local copies, waits for them, and re-layouts: 15 us -> 5.91 us
    all_gather x3 -> x0, waiting for transfers between devices: 254 us -> none  [the longest x1 128 us: carried_in(): pieces = jax.tree.map(lambda part: lax.all_gather(part, axis), value)]
    all_gather x1 -> x0, blocking collectives: 67.5 us -> none  [carried_in(): pieces = jax.tree.map(lambda part: lax.all_gather(part, axis), value)]
    pallas_call x0 -> x1, Pallas kernels: none -> 63.6 us  [per_device(): pl.pallas_call(kernel, out_shape=(jax.ShapeDtypeStruct((TOK, 4 * HD), BF1...]
    select_n x63 -> x0, other arithmetic: 54.9 us -> none  [hop(): jnp.where(position < mine, new, old)]
    psum x1 -> x0, waiting for transfers between devices: 49.6 us -> none  [mixer_layer(): summed, maps = lax.psum((part_step, part_maps), 'tp')]
    psum x2 -> x0, blocking collectives: 48.5 us -> none  [the longest x1 26.9 us: mixer_layer(): summed, maps = lax.psum((part_step, part_maps), 'tp')]
    dot_general x8 -> x0, matrix products: 13.8 us -> none  [the longest x1 4.75 us: update(): jnp.einsum('kgts,skd->kgtd', weights.astype(jnp.bfloat16), values_here, p...]
  transfers between devices with their start and end apart: 4 -> 0, of which waited for: 3 -> 0; matrix products, arithmetic and copies ran while one was open for 5% -> 0% of each run, Pallas kernels for 0% -> 0%
where the time goes in v1:
time: 70.5 us; the launch traced here: 70.2 us
  Pallas kernels  63.6 us (90%)
  local copies, waits for them, and re-layouts  5.91 us (8%)
  between operations  0.75 us (1%)
    pallas_call x1, Pallas kernels, per_device(): pl.pallas_call(kernel, out_shape=(jax.ShapeDtypeStruct((TOK, 4 * HD), BF1...  63.6 us
    unnamed x23, local copies, waits for them, and re-layouts  5.91 us

profile of v1, /device:TPU:1, one launch (start us, length us, event | category | flops | bytes accessed | tf_op | source)
XLA Modules:
  0.0 70.2 jit_solution(4044378203109763878)
XLA Ops:
  0.6 0.0 copy-start
  0.6 0.0 copy-start.4
  0.7 0.0 copy-start.5
  0.7 0.0 copy-start.7
  0.7 0.0 copy-start.8
  0.7 0.0 copy-start.9
  0.7 1.0 %copy.13.wm_ref = bf16[1024,32]{1,0:T(8,128)(2,1)S(1)} copy(bf16[1024,32]{0,1:T(8,128)(2,1)} %param.17) | data formatting | bytes 131072 | tf_op args[6]
  1.7 0.0 copy-done
  1.8 0.0 copy-done.4
  1.8 0.0 copy-done.5
  1.8 0.0 copy-done.7
  1.8 0.0 copy-done.8
  1.8 0.0 copy-done.9
  1.8 0.0 copy-start.1
  1.8 0.9 %copy-done.1 = bf16[128,1024]{1,0:T(8,128)(2,1)S(1)} copy-done((bf16[128,1024]{1,0:T(8,128)(2,1)S(1)}, bf16[128,1024]{1,0:T(8,128)(2,1)}, u32[]{:S(2)}) %copy-start.1) | copy-done | bytes 262168
  2.8 0.0 copy-start.2
  2.8 0.9 %copy-done.2 = bf16[1024,128]{1,0:T(8,128)(2,1)S(1)} copy-done((bf16[1024,128]{1,0:T(8,128)(2,1)S(1)}, bf16[1024,128]{1,0:T(8,128)(2,1)}, u32[]{:S(2)}) %copy-start.2) | copy-done | bytes 262168
  3.7 0.0 copy-start.3
  3.7 0.9 %copy-done.3 = bf16[128,512]{1,0:T(8,128)(2,1)S(1)} copy-done((bf16[128,512]{1,0:T(8,128)(2,1)S(1)}, bf16[128,512]{1,0:T(8,128)(2,1)}, u32[]{:S(2)}) %copy-start.3) | copy-done | bytes 131096
  4.6 0.0 copy-start.6
  4.6 0.7 copy-done.6
  5.3 63.6 %shard_map.122 = (bf16[128,512]{1,0:T(8,128)(2,1)S(1)}, bf16[128,1024]{1,0:T(8,128)(2,1)S(1)}) custom-call(bf16[128,512]{1,0:T(8,128)(2,1)S(1)} %copy-done.3, bf16[128,128]{1,0:T(8,128)(2,1)S(1)} %copy-done.4, bf16[128,128]{1,0:T(8,128)(2,1)S(1)} %copy-done.5, bf16[128,1024]{1,0:T(8,128)(2,1)S(1)} %copy-done, bf16[128,1024]{1,0:T(8,128)(2,1)S(1)} %copy-done.1, ...), custom_call_target="tpu_custom_call" | custom-call | tf_op jit(solution)/shard_map/pallas_call | solution.py:418
  68.9 0.7 copy.16
  69.5 0.7 copy.17
Async XLA Ops:
  0.6 1.1 %copy-start = (bf16[128,1024]{1,0:T(8,128)(2,1)S(1)}, bf16[128,1024]{1,0:T(8,128)(2,1)}, u32[]{:S(2)}) copy-start(bf16[128,1024]{1,0:T(8,128)(2,1)} %x_ref.1) | copy-start | bytes 786436
  0.6 1.1 %copy-start.4 = (bf16[128,128]{1,0:T(8,128)(2,1)S(1)}, bf16[128,128]{1,0:T(8,128)(2,1)}, u32[]{:S(2)}) copy-start(bf16[128,128]{1,0:T(8,128)(2,1)} %k_ref.1) | copy-start | bytes 98308
  0.7 1.1 %copy-start.5 = (bf16[128,128]{1,0:T(8,128)(2,1)S(1)}, bf16[128,128]{1,0:T(8,128)(2,1)}, u32[]{:S(2)}) copy-start(bf16[128,128]{1,0:T(8,128)(2,1)} %v_ref.1) | copy-start | bytes 98308
  0.7 1.1 %copy-start.7 = (f32[16]{0:T(128)S(1)}, f32[16]{0:T(128)}, u32[]{:S(2)}) copy-start(f32[16]{0:T(128)} %bias_ref.1) | copy-start | bytes 196
  0.7 1.1 %copy-start.8 = (f32[16]{0:T(128)S(1)}, f32[16]{0:T(128)}, u32[]{:S(2)}) copy-start(f32[16]{0:T(128)} %rate_ref.1) | copy-start | bytes 196
  0.7 1.1 %copy-start.9 = (f32[16]{0:T(128)S(1)}, f32[16]{0:T(128)}, u32[]{:S(2)}) copy-start(f32[16]{0:T(128)} %skip_ref.1) | copy-start | bytes 196
  1.8 1.0 %copy-start.1 = (bf16[128,1024]{1,0:T(8,128)(2,1)S(1)}, bf16[128,1024]{1,0:T(8,128)(2,1)}, u32[]{:S(2)}) copy-start(bf16[128,1024]{1,0:T(8,128)(2,1)} %gate_ref.1) | copy-start | bytes 786436
  2.8 0.9 %copy-start.2 = (bf16[1024,128]{1,0:T(8,128)(2,1)S(1)}, bf16[1024,128]{1,0:T(8,128)(2,1)}, u32[]{:S(2)}) copy-start(bf16[1024,128]{1,0:T(8,128)(2,1)} %ws_ref.1) | copy-start | bytes 786436
  3.7 0.9 %copy-start.3 = (bf16[128,512]{1,0:T(8,128)(2,1)S(1)}, bf16[128,512]{1,0:T(8,128)(2,1)}, u32[]{:S(2)}) copy-start(bf16[128,512]{1,0:T(8,128)(2,1)} %q_ref.1) | copy-start | bytes 393220
  4.6 0.7 copy-start.6

commit v2 on v1

--- a/solution.py
+++ b/solution.py
@@ -17,7 +17,7 @@
 STATE = 16
 PAIRS = 8
 CHANNELS = 8192
-SCALE = 1.0 / math.sqrt(HD)
+SCALE2 = math.log2(math.e) / math.sqrt(HD)
 F32 = jnp.float32
 BF16 = jnp.bfloat16
 EXACT = lax.Precision.HIGHEST
@@ -35,12 +35,13 @@
 
 
 def kernel(
-    q_ref, k_ref, v_ref, x_ref, gate_ref, ws_ref, wm_ref, bias_ref, rate_ref, skip_ref, norm_ref,
+    q_hbm, k_hbm, v_hbm, x_hbm, gate_hbm, ws_hbm, wm_hbm, bias_hbm, rate_hbm, skip_hbm, norm_hbm,
     attn_ref, mamba_ref,
-    kbuf, vbuf, qbuf, obuf, orecv, stat_send, stat_recv, own_out, acc_out,
+    q_ref, x_ref, gate_ref, ws_ref, wm_ref, bias_ref, rate_ref, skip_ref, norm_ref,
+    kbuf, vbuf, qbuf, obuf, orecv, stat_send, stat_recv, own_out, acc_out, part, part_stat,
     proj_send, proj_recv, csend, crecv, fsend, frecv, ysend, yrecv, rsend, srecv,
     base, gated, sqsend, sqrecv, pref,
-    ring_ss, ring_rs, q_ss, q_rs, o_ss, o_rs, st_ss, st_rs, grp_ss, grp_rs,
+    load_sem, ring_ss, ring_rs, q_ss, q_rs, o_ss, o_rs, st_ss, st_rs, grp_ss, grp_rs, known,
 ):
     me = lax.axis_index("ctx")
     t = lax.axis_index("tp")
@@ -58,25 +59,27 @@
     def at(ctx, tp):
         return {"ctx": ctx, "tp": tp}
 
+    def signal(sem, ctx, tp):
+        pl.semaphore_signal(sem, inc=1, device_id=at(ctx, tp), device_id_type=MESH)
+
     barrier = pltpu.get_barrier_semaphore()
     for o in range(1, TP):
-        pl.semaphore_signal(barrier, inc=1, device_id=at(me, tp_peer(o)), device_id_type=MESH)
-    for o in range(1, ROW):
-        pl.semaphore_signal(barrier, inc=1, device_id=at(z_peer(o), t), device_id_type=MESH)
+        signal(barrier, me, tp_peer(o))
+    for o in (1, -1):
+        signal(barrier, z_peer(o), t)
     for o in range(1, ROWS):
-        pl.semaphore_signal(barrier, inc=1, device_id=at(y_peer(o), t), device_id_type=MESH)
-
-    ws = dot(x_ref[...], ws_ref[...])
-    wm = dot(x_ref[...], wm_ref[...])
-    step_part = ws.T
-    maps_part = jnp.concatenate([wm, jnp.zeros((TOK, 96), F32)], axis=1).T[:32]
-    for p in range(TP):
-        proj_send[p, 0:16, :] = step_part[16 * p:16 * p + 16]
-        proj_send[p, 16:48, :] = maps_part
-    kbuf[z] = k_ref[...]
-    vbuf[z] = v_ref[...]
-
-    pl.semaphore_wait(barrier, TP - 1 + ROW - 1 + ROWS - 1)
+        signal(barrier, y_peer(o), t)
+
+    loads = [
+        pltpu.make_async_copy(src, dst, load_sem.at[i])
+        for i, (src, dst) in enumerate((
+            (x_hbm, x_ref), (ws_hbm, ws_ref), (wm_hbm, wm_ref), (bias_hbm, bias_ref),
+            (rate_hbm, rate_ref), (skip_hbm, skip_ref), (k_hbm, kbuf.at[4]), (v_hbm, vbuf.at[4]),
+            (q_hbm, q_ref), (gate_hbm, gate_ref), (norm_hbm, norm_ref),
+        ))
+    ]
+    for copy in loads:
+        copy.start()
 
     def remote(src, dst, ssem, rsem, ctx, tp):
         return pltpu.make_async_remote_copy(
@@ -84,21 +87,15 @@
             device_id=at(ctx, tp), device_id_type=MESH,
         )
 
-    def proj_copy(o):
-        return remote(
-            proj_send.at[tp_peer(o)], proj_recv.at[t], grp_ss.at[0], grp_rs.at[0], me, tp_peer(o)
-        )
-
-    for o in range(1, TP):
-        proj_copy(o).start()
+    pl.semaphore_wait(barrier, TP - 1 + 2 + ROWS - 1)
 
     def ring_copy(kv, d, s):
-        block = lax.rem(z - d * (s - 1) + 2 * ROW, ROW)
         buf = (kbuf, vbuf)[kv]
         i = 0 if d > 0 else 1
-        src = (k_ref, v_ref)[kv] if s == 1 else buf.at[block]
-        return remote(
-            src, buf.at[block], ring_ss.at[kv, i, s - 1], ring_rs.at[kv, i, s - 1], z_peer(d), t
+        src = (k_hbm, v_hbm)[kv] if s == 1 else buf.at[(4 - d * (s - 1)) % ROW]
+        return remote(
+            src, buf.at[(4 - d * s) % ROW], ring_ss.at[kv, i, s - 1], ring_rs.at[kv, i, s - 1],
+            z_peer(d), t,
         )
 
     def ring_steps(d):
@@ -107,6 +104,8 @@
     for kv in (0, 1):
         for d in (1, -1):
             ring_copy(kv, d, 1).start()
+    for o in (1, -1):
+        signal(known.at[0], z_peer(o), t)
 
     def ring(s):
         for kv in (0, 1):
@@ -117,12 +116,28 @@
                         ring_copy(kv, d, s + 1).start()
 
     def q_copy(o):
-        return remote(q_ref, qbuf.at[o - 1], q_ss.at[o - 1], q_rs.at[o - 1], y_peer(-o), t)
+        return remote(q_hbm, qbuf.at[o - 1], q_ss.at[o - 1], q_rs.at[o - 1], y_peer(-o), t)
 
     for o in range(1, ROWS):
         @pl.when(y >= o)
         def _(o=o):
             q_copy(o).start()
+
+    for copy in loads[:6]:
+        copy.wait()
+    step_part = dot(x_ref[...], ws_ref[...]).T
+    maps_part = dot_t(wm_ref[...], x_ref[...])
+    for p in range(TP):
+        proj_send[p, 0:16, :] = step_part[16 * p:16 * p + 16]
+        proj_send[p, 16:48, :] = maps_part
+
+    def proj_copy(o):
+        return remote(
+            proj_send.at[tp_peer(o)], proj_recv.at[t], grp_ss.at[0], grp_rs.at[0], me, tp_peer(o)
+        )
+
+    for o in range(1, TP):
+        proj_copy(o).start()
 
     lane = lax.broadcasted_iota(jnp.int32, (TOK, TOK), 1)
     sub = lax.broadcasted_iota(jnp.int32, (TOK, TOK), 0)
@@ -137,7 +152,15 @@
         return out
 
     bias, rate = column(bias_ref), column(rate_ref)
+    pl.semaphore_wait(known.at[0], 2)
+    for o in (2, -2):
+        signal(known.at[1], z_peer(o), t)
+
     ring(1)
+    pl.semaphore_wait(known.at[1], 2)
+    for o in (4, -4):
+        signal(known.at[2], z_peer(o), t)
+    ring(2)
 
     remote(
         proj_send.at[0:TP - 1], proj_recv.at[0:TP - 1], grp_ss.at[0], grp_rs.at[0], me, tp_peer(1)
@@ -155,14 +178,6 @@
     final = jnp.broadcast_to(climb[:, TOK - 1:TOK], (HEADS, TOK))
     for j in range(PAIRS):
         fsend[j] = jnp.where(low[0:1], final[2 * j:2 * j + 1], final[2 * j + 1:2 * j + 2])
-    def f_copy(o):
-        return remote(
-            fsend.at[lax.rem(z + o, ROW) // 2], frecv.at[z], grp_ss.at[1], grp_rs.at[1],
-            z_peer(o), t,
-        )
-
-    for o in range(1, ROW):
-        f_copy(o).start()
     feed_weight = jnp.exp(final - climb) * step
 
     def pair_input(j):
@@ -178,17 +193,25 @@
         csend[2 * j] = contrib[0:8]
         csend[2 * j + 1] = contrib[8:16]
 
+    pl.semaphore_wait(known.at[2], 2)
+
+    def f_copy(o):
+        return remote(
+            fsend.at[lax.rem(z + o, ROW) // 2], frecv.at[z], grp_ss.at[1], grp_rs.at[1],
+            z_peer(o), t,
+        )
+
     def c_copy(o):
         return remote(
             csend.at[lax.rem(z + o, ROW)], crecv.at[z], grp_ss.at[2], grp_rs.at[2], z_peer(o), t
         )
 
-    for o in range(1, ROW):
+    for o in (8, 7, 9, 6, 10, 5, 11, 4, 12, 3, 13, 2, 14, 1, 15):
+        f_copy(o).start()
         c_copy(o).start()
     crecv[z] = csend[z]
     frecv[z] = fsend[z // 2]
-    ring(2)
-
+    ring(3)
     turned = jnp.concatenate([c_rows, climb, jnp.exp(climb), jnp.zeros((80, TOK), F32)], axis=0).T
     c_cols = turned[:, 0:16]
     inner = dot(c_cols, b_rows, EXACT)
@@ -205,19 +228,68 @@
         cols = slice(128 * j, 128 * j + 128)
         base[:, cols] = out + gain * x_ref[:, cols].astype(F32)
 
-    for j in range(4):
+    for j in range(PAIRS):
         local_pair(j)
-    ring(3)
-    for j in range(4, PAIRS):
-        local_pair(j)
+
+    half_keys = 8 * TOK
+    slot = lax.broadcasted_iota(jnp.int32, (1, half_keys), 1)
+    query_row = lax.broadcasted_iota(jnp.int32, (2 * TOK, 1), 0)
+    query_row = jnp.where(query_row >= TOK, query_row - TOK, query_row) + z * TOK
+    lane2 = lax.broadcasted_iota(jnp.int32, (2 * TOK, TOK), 1)
+
+    def scores_of(o, pair, side):
+        src = q_ref if o == 0 else qbuf.at[o - 1]
+        q = jnp.concatenate(
+            [src[:, 128 * h:128 * h + 128] for h in (2 * pair, 2 * pair + 1)], axis=0
+        )
+        out = dot_t(q, kbuf[8 * side:8 * side + 8].reshape(half_keys, HD))
+        if o == 0:
+            block = lax.rem(slot // TOK + (z + 8 * side - 4 + ROW), ROW)
+            out = jnp.where(block * TOK + slot % TOK <= query_row, out, -1e30)
+        return out
+
+    def first_half(o, pair):
+        scores = scores_of(o, pair, 0)
+        top = jnp.max(scores, axis=1, keepdims=True)
+        weights = jnp.exp2((scores - top) * SCALE2)
+        whole = jnp.sum(weights, axis=1, keepdims=True)
+        part[o, pair] = dot(weights.astype(BF16), vbuf[0:8].reshape(half_keys, HD))
+        part_stat[o, pair] = jnp.where(lane2 == 0, top, whole)
+
+    def second_half(o, pair):
+        scores = scores_of(o, pair, 1)
+        stat = part_stat[o, pair]
+        before = stat[:, 0:1]
+        top = jnp.maximum(before, jnp.max(scores, axis=1, keepdims=True))
+        weights = jnp.exp2((scores - top) * SCALE2)
+        keep = jnp.exp2((before - top) * SCALE2)
+        whole = stat[:, 1:2] * keep + jnp.sum(weights, axis=1, keepdims=True)
+        mixed = part[o, pair] * keep + dot(
+            weights.astype(BF16), vbuf[8:16].reshape(half_keys, HD)
+        )
+        return mixed / whole, top, whole
+
+    def first_halves(o):
+        @pl.when(y + o < ROWS)
+        def _():
+            if o:
+                q_copy(o).wait_recv()
+            for pair in (0, 1):
+                first_half(o, pair)
+
+    for copy in loads[6:]:
+        copy.wait()
     ring(4)
+    first_halves(1)
     ring(5)
 
+    first_halves(2)
+    ring(6)
+    remote(
+        frecv.at[0:ROW - 1], frecv.at[0:ROW - 1], grp_ss.at[1], grp_rs.at[1], z_peer(1), t
+    ).wait_recv()
     remote(
         csend.at[0:ROW - 1], crecv.at[0:ROW - 1], grp_ss.at[2], grp_rs.at[2], z_peer(1), t
-    ).wait_recv()
-    remote(
-        frecv.at[0:ROW - 1], frecv.at[0:ROW - 1], grp_ss.at[1], grp_rs.at[1], z_peer(1), t
     ).wait_recv()
     running = jnp.zeros((8, TOK), F32)
     passed = jnp.zeros((1, TOK), F32)
@@ -233,10 +305,11 @@
     def y_copy(o):
         return remote(ysend, yrecv.at[y], grp_ss.at[3], grp_rs.at[3], y_peer(o), t)
 
-    for o in range(1, ROWS):
+    for o in (2, 1, 3):
         y_copy(o).start()
     yrecv[y] = ysend[...]
-    ring(6)
+    first_halves(3)
+    ring(7)
     remote(
         yrecv.at[0:ROWS - 1], yrecv.at[0:ROWS - 1], grp_ss.at[3], grp_rs.at[3], y_peer(1), t
     ).wait_recv()
@@ -252,28 +325,11 @@
             rsend.at[lax.rem(z + o, ROW)], srecv.at[z], grp_ss.at[4], grp_rs.at[4], z_peer(o), t
         )
 
-    for o in range(1, ROW):
+    for o in (8, 7, 9, 6, 10, 5, 11, 4, 12, 3, 13, 2, 14, 1, 15):
         r_copy(o).start()
     srecv[z] = rsend[z]
-    ring(7)
+    first_halves(0)
     ring(8)
-
-    keys = ROW * TOK
-
-    def unit(q, masked):
-        scores = dot_t(q, kbuf[...].reshape(keys, HD)) * SCALE
-        if masked:
-            key = lax.broadcasted_iota(jnp.int32, (TOK, keys), 1)
-            query = lax.broadcasted_iota(jnp.int32, (TOK, keys), 0) + z * TOK
-            mask = key <= query
-            scores = jnp.where(mask, scores, -1e30)
-        top = jnp.max(scores, axis=1, keepdims=True)
-        weights = jnp.exp(scores - top)
-        if masked:
-            weights = jnp.where(mask, weights, 0.0)
-        whole = jnp.sum(weights, axis=1, keepdims=True)
-        mixed = dot(weights.astype(BF16), vbuf[...].reshape(keys, HD))
-        return mixed / whole, top, whole
 
     def stats_of(tops, wholes):
         out = jnp.zeros((TOK, TOK), F32)
@@ -281,11 +337,10 @@
             out = jnp.where(lane == i, col, out)
         return out
 
-    def o_copy(o, h):
-        cols = slice(128 * h, 128 * h + 128)
-        return remote(
-            obuf.at[o - 1, h], orecv.at[o - 1, h],
-            o_ss.at[o - 1, h], o_rs.at[o - 1, h], y_peer(o), t,
+    def o_copy(o, pair):
+        return remote(
+            obuf.at[o - 1, pair], orecv.at[o - 1, pair],
+            o_ss.at[o - 1, pair], o_rs.at[o - 1, pair], y_peer(o), t,
         )
 
     def st_copy(o):
@@ -297,23 +352,23 @@
     for o in (3, 2, 1):
         @pl.when(y + o < ROWS)
         def _(o=o):
-            q_copy(o).wait_recv()
             tops, wholes = [], []
-            for h in range(4):
-                mixed, top, whole = unit(qbuf[o - 1, :, 128 * h:128 * h + 128], False)
-                obuf[o - 1, h] = mixed.astype(BF16)
-                o_copy(o, h).start()
-                tops.append(top)
-                wholes.append(whole)
+            for pair in (0, 1):
+                mixed, top, whole = second_half(o, pair)
+                obuf[o - 1, pair] = mixed.astype(BF16)
+                o_copy(o, pair).start()
+                tops += [top[0:TOK], top[TOK:]]
+                wholes += [whole[0:TOK], whole[TOK:]]
             stat_send[o - 1] = stats_of(tops, wholes).T[0:8]
             st_copy(o).start()
 
     tops, wholes = [], []
-    for h in range(4):
-        mixed, top, whole = unit(q_ref[:, 128 * h:128 * h + 128], True)
-        acc_out[:, 128 * h:128 * h + 128] = mixed
-        tops.append(top)
-        wholes.append(whole)
+    for pair in (0, 1):
+        mixed, top, whole = second_half(0, pair)
+        acc_out[:, 256 * pair:256 * pair + 128] = mixed[0:TOK]
+        acc_out[:, 256 * pair + 128:256 * pair + 256] = mixed[TOK:]
+        tops += [top[0:TOK], top[TOK:]]
+        wholes += [whole[0:TOK], whole[TOK:]]
     own_out[...] = stats_of(tops, wholes)
 
     remote(
@@ -346,16 +401,18 @@
             mine = own_out[...]
             tops, wholes = [], []
             for h in range(4):
-                o_copy(o, h).wait_recv()
+                if h % 2 == 0:
+                    o_copy(o, h // 2).wait_recv()
                 cols = slice(128 * h, 128 * h + 128)
+                rows = slice(128 * (h % 2), 128 * (h % 2) + 128)
                 top_a, top_b = mine[:, h:h + 1], other[:, h:h + 1]
                 top = jnp.maximum(top_a, top_b)
-                part_a = mine[:, 4 + h:5 + h] * jnp.exp(top_a - top)
-                part_b = other[:, 4 + h:5 + h] * jnp.exp(top_b - top)
+                part_a = mine[:, 4 + h:5 + h] * jnp.exp2((top_a - top) * SCALE2)
+                part_b = other[:, 4 + h:5 + h] * jnp.exp2((top_b - top) * SCALE2)
                 whole = part_a + part_b
                 acc_out[:, cols] = (
                     acc_out[:, cols] * (part_a / whole)
-                    + orecv[o - 1, h].astype(F32) * (part_b / whole)
+                    + orecv[o - 1, h // 2, rows].astype(F32) * (part_b / whole)
                 )
                 tops.append(top)
                 wholes.append(whole)
@@ -404,8 +461,8 @@
 
         @pl.when(y + o < ROWS)
         def _(o=o):
-            for h in range(4):
-                o_copy(o, h).wait_send()
+            for pair in (0, 1):
+                o_copy(o, pair).wait_send()
             st_copy(o).wait_send()
 
 
@@ -414,25 +471,36 @@
     skip_gain, norm_gain,
 ):
     vmem = pl.BlockSpec(memory_space=pltpu.VMEM)
-    smem = pl.BlockSpec(memory_space=pltpu.SMEM)
+    hbm = pl.BlockSpec(memory_space=pltpu.HBM)
     return pl.pallas_call(
         kernel,
         out_shape=(
             jax.ShapeDtypeStruct((TOK, 4 * HD), BF16),
             jax.ShapeDtypeStruct((TOK, 1024), BF16),
         ),
-        in_specs=[vmem] * 7 + [smem] * 3 + [vmem],
+        in_specs=[hbm] * 11,
         out_specs=(vmem, vmem),
         scratch_shapes=[
+            pltpu.VMEM((TOK, 4 * HD), BF16),
+            pltpu.VMEM((TOK, 1024), BF16),
+            pltpu.VMEM((TOK, 1024), BF16),
+            pltpu.VMEM((1024, 128), BF16),
+            pltpu.VMEM((32, 1024), BF16),
+            pltpu.SMEM((HEADS,), F32),
+            pltpu.SMEM((HEADS,), F32),
+            pltpu.SMEM((HEADS,), F32),
+            pltpu.VMEM((1, 1024), F32),
             pltpu.VMEM((ROW, TOK, HD), BF16),
             pltpu.VMEM((ROW, TOK, HD), BF16),
             pltpu.VMEM((3, TOK, 4 * HD), BF16),
-            pltpu.VMEM((3, 4, TOK, HD), BF16),
-            pltpu.VMEM((3, 4, TOK, HD), BF16),
+            pltpu.VMEM((3, 2, 2 * TOK, HD), BF16),
+            pltpu.VMEM((3, 2, 2 * TOK, HD), BF16),
             pltpu.VMEM((3, 8, TOK), F32),
             pltpu.VMEM((3, 8, TOK), F32),
             pltpu.VMEM((TOK, TOK), F32),
             pltpu.VMEM((TOK, 4 * HD), F32),
+            pltpu.VMEM((4, 2, 2 * TOK, HD), F32),
+            pltpu.VMEM((4, 2, 2 * TOK, TOK), F32),
             pltpu.VMEM((TP, 48, TOK), F32),
             pltpu.VMEM((TP, 48, TOK), F32),
             pltpu.VMEM((ROW, 8, TOK), F32),
@@ -448,24 +516,26 @@
             pltpu.VMEM((8, TOK), F32),
             pltpu.VMEM((TP, 8, TOK), F32),
             pltpu.VMEM((ROW, 8, TOK), F32),
+            pltpu.SemaphoreType.DMA((11,)),
             pltpu.SemaphoreType.DMA((2, 2, 8)),
             pltpu.SemaphoreType.DMA((2, 2, 8)),
             pltpu.SemaphoreType.DMA((3,)),
             pltpu.SemaphoreType.DMA((3,)),
-            pltpu.SemaphoreType.DMA((3, 4)),
-            pltpu.SemaphoreType.DMA((3, 4)),
+            pltpu.SemaphoreType.DMA((3, 2)),
+            pltpu.SemaphoreType.DMA((3, 2)),
             pltpu.SemaphoreType.DMA((3,)),
             pltpu.SemaphoreType.DMA((3,)),
             pltpu.SemaphoreType.DMA((6,)),
             pltpu.SemaphoreType.DMA((6,)),
+            pltpu.SemaphoreType.REGULAR((3,)),
         ],
         compiler_params=pltpu.CompilerParams(
             collective_id=0, has_side_effects=True, vmem_limit_bytes=48 << 20
         ),
-    )(
-        queries, keys, values, mixer_input, gate, step_weight, state_weight, step_bias,
+    )(*[pltpu.with_memory_space_constraint(a, pltpu.HBM) for a in (
+        queries, keys, values, mixer_input, gate, step_weight, state_weight.T, step_bias,
         decay_rate, skip_gain, norm_gain.reshape(1, -1),
-    )
+    )])
 
 
 def solution(mesh):

time: 70.5 us -> 56.7 us (0.80)
  Pallas kernels: 63.6 us -> 54.6 us
  local copies, waits for them, and re-layouts: 5.91 us -> 1.36 us
    pallas_call x1, Pallas kernels: 63.6 us -> 54.6 us  [per_device(): pl.pallas_call(kernel, out_shape=(jax.ShapeDtypeStruct((TOK, 4 * HD), BF1...]
    unnamed x23 -> x2, local copies, waits for them, and re-layouts: 5.91 us -> 1.36 us
where the time goes in v2:
time: 56.7 us; the launch traced here: 56.6 us
  Pallas kernels  54.6 us (96%)
  local copies, waits for them, and re-layouts  1.36 us (2%)
  between operations  0.64 us (1%)
    pallas_call x1, Pallas kernels, per_device(): pl.pallas_call(kernel, out_shape=(jax.ShapeDtypeStruct((TOK, 4 * HD), BF1...  54.6 us
    unnamed x2, local copies, waits for them, and re-layouts  1.36 us

profile of v2, /device:TPU:1, one launch (start us, length us, event | category | flops | bytes accessed | tf_op | source)
XLA Modules:
  0.0 56.6 jit_solution(12912381025596060081)
XLA Ops:
  0.6 54.6 %shard_map.122 = (bf16[128,512]{1,0:T(8,128)(2,1)S(1)}, bf16[128,1024]{1,0:T(8,128)(2,1)S(1)}) custom-call(bf16[128,512]{1,0:T(8,128)(2,1)} %q_hbm.1, bf16[128,128]{1,0:T(8,128)(2,1)} %k_hbm.1, bf16[128,128]{1,0:T(8,128)(2,1)} %v_hbm.1, bf16[128,1024]{1,0:T(8,128)(2,1)} %x_hbm.1, bf16[128,1024]{1,0:T(8,128)(2,1)} %gate_hbm.1, bf16[1024,128]{1,0:T(8,128)(2,1)} %ws_hbm.1, ...), custom_call_target="tpu_custom_call" | custom-call | tf_op jit(solution)/shard_map/pallas_call | solution.py:475
  55.2 0.7 %copy.15 = bf16[128,512]{1,0:T(8,128)(2,1)} copy(bf16[128,512]{1,0:T(8,128)(2,1)S(1)} %get-tuple-element.4) | data formatting | bytes 262144
  55.9 0.7 %copy.16 = bf16[128,1024]{1,0:T(8,128)(2,1)} copy(bf16[128,1024]{1,0:T(8,128)(2,1)S(1)} %get-tuple-element.5) | data formatting | bytes 524288

commit v3 on v2

v3 whole, which is shorter than its diff:
```python
import functools
import math

import jax
import jax.numpy as jnp
from jax import lax
from jax.experimental import pallas as pl
from jax.experimental.pallas import tpu as pltpu
from jax.sharding import PartitionSpec as P

HD = 128
TOK = 128
ROW = 16
ROWS = 4
TP = 8
HEADS = 16
STATE = 16
PAIRS = 8
CHANNELS = 8192
SCALE2 = math.log2(math.e) / math.sqrt(HD)
F32 = jnp.float32
BF16 = jnp.bfloat16
EXACT = lax.Precision.HIGHEST
MESH = pl.DeviceIdType.MESH


SLOTS = (-2, -1, 0, 1, 2, 3, 4, -3, -4, 5, 6, -5, -6, 7, -7, -8)
PARTS = ((0, 5), (5, 9), (9, 13), (13, 16))


def slot_of(r):
    return SLOTS.index(r)


def dot(a, b, precision=None):
    return jnp.dot(a, b, preferred_element_type=F32, precision=precision)


def dot_t(a, b, precision=None):
    return lax.dot_general(
        a, b, (((1,), (1,)), ((), ())), preferred_element_type=F32, precision=precision
    )


def kernel(
    q_hbm, k_hbm, v_hbm, x_hbm, gate_hbm, ws_hbm, wm_hbm, bias_hbm, rate_hbm, skip_hbm, norm_hbm,
    attn_ref, mamba_ref,
    q_ref, x_ref, gate_ref, ws_ref, wm_ref, bias_ref, rate_ref, skip_ref, norm_ref,
    kbuf, vbuf, qbuf, obuf, orecv, stat_send, stat_recv, part, part_stat,
    proj_send, proj_recv, csend, crecv, fsend, frecv, ysend, yrecv, rsend, srecv,
    base, gated, sqsend, sqrecv, pref,
    load_sem, ring_ss, ring_rs, q_ss, q_rs, o_ss, o_rs, st_ss, st_rs, y_ss, y_rs, grp_ss, grp_rs, known,
):
    me = lax.axis_index("ctx")
    t = lax.axis_index("tp")
    y, z = me // ROW, me % ROW

    def tp_peer(o):
        return lax.rem(t + o, TP)

    def z_peer(o):
        return y * ROW + lax.rem(z + o + ROW, ROW)

    def y_peer(o):
        return lax.rem(y + o + ROWS, ROWS) * ROW + z

    def at(ctx, tp):
        return {"ctx": ctx, "tp": tp}

    def signal(sem, ctx, tp):
        pl.semaphore_signal(sem, inc=1, device_id=at(ctx, tp), device_id_type=MESH)

    barrier = pltpu.get_barrier_semaphore()
    for o in range(1, TP):
        signal(barrier, me, tp_peer(o))
    for o in (1, -1):
        signal(barrier, z_peer(o), t)
    for o in range(1, ROWS):
        signal(barrier, y_peer(o), t)

    loads = [
        pltpu.make_async_copy(src, dst, load_sem.at[i])
        for i, (src, dst) in enumerate((
            (x_hbm, x_ref), (ws_hbm, ws_ref), (wm_hbm, wm_ref), (bias_hbm, bias_ref),
            (rate_hbm, rate_ref), (skip_hbm, skip_ref), (k_hbm, kbuf.at[slot_of(0)]), (v_hbm, vbuf.at[slot_of(0)]),
            (q_hbm, q_ref), (gate_hbm, gate_ref), (norm_hbm, norm_ref),
        ))
    ]
    for copy in loads:
        copy.start()

    def remote(src, dst, ssem, rsem, ctx, tp):
        return pltpu.make_async_remote_copy(
            src_ref=src, dst_ref=dst, send_sem=ssem, recv_sem=rsem,
            device_id=at(ctx, tp), device_id_type=MESH,
        )

    pl.semaphore_wait(barrier, TP - 1 + 2 + ROWS - 1)

    def ring_copy(kv, d, s):
        buf = (kbuf, vbuf)[kv]
        i = 0 if d > 0 else 1
        src = (k_hbm, v_hbm)[kv] if s == 1 else buf.at[slot_of(-d * (s - 1))]
        return remote(
            src, buf.at[slot_of(-d * s)], ring_ss.at[kv], ring_rs.at[kv, i, s - 1], z_peer(d), t
        )

    def ring_steps(d):
        return ROW // 2 if d > 0 else ROW // 2 - 1

    pieces = [(kv, d) for kv in (0, 1) for d in (1, -1)]
    for kv, d in pieces:
        ring_copy(kv, d, 1).start()
    for o in (1, -1):
        signal(known.at[0], z_peer(o), t)

    def ring(s):
        for kv, d in pieces:
            if s <= ring_steps(d):
                ring_copy(kv, d, s).wait_recv()
                if s + 1 <= ring_steps(d):
                    ring_copy(kv, d, s + 1).start()

    def q_copy(o):
        return remote(q_hbm, qbuf.at[o - 1], q_ss.at[o - 1], q_rs.at[o - 1], y_peer(-o), t)

    for o in range(1, ROWS):
        @pl.when(y >= o)
        def _(o=o):
            q_copy(o).start()

    for copy in loads[:6]:
        copy.wait()
    step_part = dot(x_ref[...], ws_ref[...]).T
    maps_part = dot_t(wm_ref[...], x_ref[...])
    for p in range(TP):
        proj_send[p, 0:16, :] = step_part[16 * p:16 * p + 16]
        proj_send[p, 16:48, :] = maps_part

    def proj_copy(o):
        return remote(
            proj_send.at[tp_peer(o)], proj_recv.at[t], grp_ss.at[0], grp_rs.at[0], me, tp_peer(o)
        )

    for o in range(1, TP):
        proj_copy(o).start()

    lane = lax.broadcasted_iota(jnp.int32, (TOK, TOK), 1)
    sub = lax.broadcasted_iota(jnp.int32, (TOK, TOK), 0)
    low = lane < 64
    sub16 = lax.broadcasted_iota(jnp.int32, (HEADS, TOK), 0)
    lane16 = lax.broadcasted_iota(jnp.int32, (HEADS, TOK), 1)

    def column(ref):
        out = jnp.full((HEADS, TOK), ref[0], F32)
        for h in range(1, HEADS):
            out = jnp.where(sub16 == h, ref[h], out)
        return out

    bias, rate = column(bias_ref), column(rate_ref)
    pl.semaphore_wait(known.at[0], 2)
    for o in (2, -2):
        signal(known.at[1], z_peer(o), t)


    def greet_far():
        pl.semaphore_wait(known.at[1], 2)
        for o in (4, -4):
            signal(known.at[2], z_peer(o), t)

    pl.when(z >= 6)(greet_far)
    ring(1)
    ring(2)

    remote(
        proj_send.at[0:TP - 1], proj_recv.at[0:TP - 1], grp_ss.at[0], grp_rs.at[0], me, tp_peer(1)
    ).wait_recv()
    proj_recv[t] = proj_send[t]
    total = proj_recv[0]
    for p in range(1, TP):
        total = total + proj_recv[p]
    b_rows, c_rows = total[16:32], total[32:48]
    raw = total[0:16] + bias
    step = jnp.maximum(raw, 0.0) + jnp.log1p(jnp.exp(-jnp.abs(raw)))
    climb = -rate * step
    for sh in (1, 2, 4, 8, 16, 32, 64):
        climb = climb + jnp.where(lane16 >= sh, pltpu.roll(climb, sh, axis=1), 0.0)
    final = jnp.broadcast_to(climb[:, TOK - 1:TOK], (HEADS, TOK))
    for j in range(PAIRS):
        fsend[j] = jnp.where(low[0:1], final[2 * j:2 * j + 1], final[2 * j + 1:2 * j + 2])
    feed_weight = jnp.exp(final - climb) * step

    def pair_input(j):
        xp = x_ref[:, 128 * j:128 * j + 128]
        zero = jnp.zeros_like(xp)
        return jnp.concatenate([jnp.where(low, xp, zero), jnp.where(low, zero, xp)], axis=0)

    for j in range(PAIRS):
        feed = jnp.concatenate(
            [b_rows * feed_weight[h:h + 1] for h in (2 * j, 2 * j + 1)], axis=1
        ).astype(BF16)
        csend[j] = dot(feed, pair_input(j)).astype(BF16)

    pl.when(z < 6)(greet_far)
    pl.semaphore_wait(known.at[2], 2)

    def f_copy(o):
        return remote(
            fsend.at[lax.rem(z + o, PAIRS)], frecv.at[z], grp_ss.at[1], grp_rs.at[1],
            z_peer(o), t,
        )

    def c_copy(o):
        return remote(
            csend.at[lax.rem(z + o, PAIRS)], crecv.at[z], grp_ss.at[2], grp_rs.at[2], z_peer(o), t
        )

    for o in (8, 7, 9, 6, 10, 5, 11, 4, 12, 3, 13, 2, 14, 1, 15):
        f_copy(o).start()
        c_copy(o).start()
    crecv[z] = csend[lax.rem(z, PAIRS)]
    frecv[z] = fsend[lax.rem(z, PAIRS)]
    ring(3)
    turned = jnp.concatenate([c_rows, climb, jnp.exp(climb), jnp.zeros((80, TOK), F32)], axis=0).T
    c_cols = turned[:, 0:16]
    inner = dot(c_cols, b_rows, EXACT)
    causal = sub >= lane

    def local_pair(j):
        mixes = []
        for h in (2 * j, 2 * j + 1):
            diff = turned[:, 16 + h:17 + h] - climb[h:h + 1]
            mix = inner * jnp.exp(diff) * step[h:h + 1]
            mixes.append(jnp.where(causal, mix, 0.0).astype(BF16))
        out = dot(jnp.concatenate(mixes, axis=1), pair_input(j))
        gain = jnp.where(low, skip_ref[2 * j], skip_ref[2 * j + 1])
        cols = slice(128 * j, 128 * j + 128)
        base[:, cols] = out + gain * x_ref[:, cols].astype(F32)

    for j in range(PAIRS):
        local_pair(j)

    query_row = lax.broadcasted_iota(jnp.int32, (4 * TOK, 1), 0) % TOK + z * TOK

    def attend(o, number):
        first, last = PARTS[number]
        src = q_ref if o == 0 else qbuf.at[o - 1]
        q = jnp.concatenate([src[:, 128 * h:128 * h + 128] for h in range(4)], axis=0)
        width = (last - first) * TOK
        scores = dot_t(q, kbuf[first:last].reshape(width, HD))
        blocks = [scores[:, TOK * i:TOK * i + TOK] for i in range(last - first)]
        if o == 0:
            place = lax.broadcasted_iota(jnp.int32, (1, TOK), 1)
            blocks = [
                jnp.where(
                    place + lax.rem(z + SLOTS[first + i] + ROW, ROW) * TOK <= query_row, b, -1e30
                )
                for i, b in enumerate(blocks)
            ]
        top = blocks[0]
        for b in blocks[1:]:
            top = jnp.maximum(top, b)
        top = jnp.broadcast_to(jnp.max(top, axis=1, keepdims=True), (4 * TOK, TOK))
        if number:
            before = part_stat[o]
            top = jnp.maximum(before, top)
        weights = jnp.concatenate(
            [jnp.exp2((b - top) * SCALE2).astype(BF16) for b in blocks], axis=1
        )
        held = vbuf[first:last].reshape(width, HD)
        mixed = dot(weights, jnp.concatenate([held, jnp.ones_like(held)], axis=1))
        if number:
            keep = jnp.exp2((before - top) * SCALE2)
            mixed = mixed + part[o] * jnp.concatenate([keep, keep], axis=1)
        if number == 3 and o:
            whole = mixed[:, HD:]
            obuf[o - 1] = (mixed[:, 0:HD] / whole).astype(BF16)
            stats = jnp.zeros((TOK, TOK), F32)
            for h in range(4):
                rows = slice(TOK * h, TOK * h + TOK)
                stats = jnp.where(lane == h, top[rows], stats)
                stats = jnp.where(lane == 4 + h, whole[rows], stats)
            stat_send[o - 1] = stats.T[0:8]
            return
        part[o] = mixed
        part_stat[o] = top

    def attend_some(number, *queries):
        for row in range(ROWS):
            mine = [o for o in queries if row + o < ROWS]
            if mine:
                @pl.when(y == row)
                def _(mine=mine):
                    if not number:
                        for o in mine:
                            if o:
                                q_copy(o).wait_recv()
                    for o in mine:
                        attend(o, number)

    for copy in loads[6:]:
        copy.wait()
    attend_some(0, 1, 2, 3, 0)
    ring(4)
    attend_some(1, 1, 2)
    remote(
        frecv.at[0:ROW - 1], frecv.at[0:ROW - 1], grp_ss.at[1], grp_rs.at[1], z_peer(1), t
    ).wait_recv()
    remote(
        crecv.at[0:ROW - 1], crecv.at[0:ROW - 1], grp_ss.at[2], grp_rs.at[2], z_peer(1), t
    ).wait_recv()
    running = jnp.zeros((STATE, TOK), F32)
    passed = jnp.zeros((1, TOK), F32)
    gone = []
    for b in range(ROW):
        pref[b] = running
        gone.append(passed)
        running = jnp.exp(frecv[b]) * running + crecv[b].astype(F32)
        passed = passed + frecv[b]
    ysend[0:16] = running
    ysend[16:24] = jnp.broadcast_to(passed, (8, TOK))

    def y_copy(o):
        return remote(ysend, yrecv.at[o - 1], y_ss.at[o - 1], y_rs.at[o - 1], y_peer(o), t)

    for o in range(1, ROWS):
        @pl.when(y + o < ROWS)
        def _(o=o):
            y_copy(o).start()

    ring(5)

    attend_some(1, 3, 0)
    for o in range(1, ROWS):
        @pl.when(y >= o)
        def _(o=o):
            y_copy(o).wait_recv()

        @pl.when(y < o)
        def _(o=o):
            yrecv[o - 1] = jnp.zeros((24, TOK), F32)

    enter = jnp.zeros((STATE, TOK), F32)
    for o in (3, 2, 1):
        enter = jnp.exp(yrecv[o - 1, 16:17]) * enter + yrecv[o - 1, 0:16]
    for b in range(ROW):
        rsend[b] = pref[b] + jnp.exp(gone[b]) * enter

    def r_copy(o):
        return remote(
            rsend.at[lax.rem(z + o + ROW, ROW)], srecv.at[lax.rem(z, PAIRS)],
            grp_ss.at[4], grp_rs.at[4], z_peer(o), t,
        )

    for o in (-4, 3, -3, 2, -2, 1, -1):
        r_copy(o).start()
    srecv[lax.rem(z, PAIRS)] = rsend[z]
    ring(6)
    attend_some(2, 3, 2)
    ring(7)
    attend_some(2, 1, 0)
    ring(8)

    def o_copy(o):
        return remote(
            obuf.at[o - 1], orecv.at[o - 1], o_ss.at[o - 1], o_rs.at[o - 1], y_peer(o), t
        )

    def st_copy(o):
        return remote(
            stat_send.at[o - 1], stat_recv.at[o - 1], st_ss.at[o - 1], st_rs.at[o - 1],
            y_peer(o), t,
        )

    attend_some(3, 3, 2, 1)
    for o in (3, 2, 1):
        @pl.when(y + o < ROWS)
        def _(o=o):
            o_copy(o).start()
            st_copy(o).start()

    remote(
        srecv.at[0:PAIRS - 1], srecv.at[0:PAIRS - 1], grp_ss.at[4], grp_rs.at[4], z_peer(1), t
    ).wait_recv()
    squares = jnp.zeros((TOK, TOK), F32)
    for j in range(PAIRS):
        cols = slice(128 * j, 128 * j + 128)
        state = srecv[j]
        grown = jnp.where(low, turned[:, 32 + 2 * j:33 + 2 * j], turned[:, 33 + 2 * j:34 + 2 * j])
        out = base[:, cols] + grown * dot(c_cols, state, EXACT)
        g = gate_ref[:, cols].astype(F32)
        out = out * (g / (1.0 + jnp.exp(-g)))
        gated[:, cols] = out
        squares = squares + out * out
    sqsend[...] = dot_t(jnp.ones((8, TOK), F32), squares, EXACT)

    def sq_copy(o):
        return remote(sqsend, sqrecv.at[t], grp_ss.at[5], grp_rs.at[5], me, tp_peer(o))

    for o in range(1, TP):
        sq_copy(o).start()
    sqrecv[t] = sqsend[...]

    attend(0, 3)
    for o in range(1, ROWS):
        @pl.when(y >= o)
        def _(o=o):
            st_copy(o).wait_recv()
            o_copy(o).wait_recv()
            other = jnp.concatenate([stat_recv[o - 1], jnp.zeros((120, TOK), F32)], axis=0).T
            for h in range(4):
                rows = slice(TOK * h, TOK * h + TOK)
                before, theirs = part_stat[0, rows], other[:, h:h + 1]
                top = jnp.maximum(before, theirs)
                keep = jnp.exp2((before - top) * SCALE2)
                gain = other[:, 4 + h:5 + h] * jnp.exp2((theirs - top) * SCALE2)
                part[0, rows, 0:HD] = (
                    part[0, rows, 0:HD] * keep + orecv[o - 1, rows].astype(F32) * gain
                )
                part[0, rows, HD:] = part[0, rows, HD:] * keep + gain
                part_stat[0, rows] = top

    for h in range(4):
        rows = slice(TOK * h, TOK * h + TOK)
        attn_ref[:, rows] = (part[0, rows, 0:HD] / part[0, rows, HD:]).astype(BF16)

    remote(
        sqrecv.at[0:TP - 1], sqrecv.at[0:TP - 1], grp_ss.at[5], grp_rs.at[5], me, tp_peer(1)
    ).wait_recv()
    square = sqrecv[0]
    for p in range(1, TP):
        square = square + sqrecv[p]
    inverse = lax.rsqrt(square[0:1] / CHANNELS + 1e-5)
    inverse = jnp.broadcast_to(inverse, (TOK, TOK)).T
    for j in range(PAIRS):
        cols = slice(128 * j, 128 * j + 128)
        mamba_ref[:, cols] = (gated[:, cols] * inverse * norm_ref[0:1, cols]).astype(BF16)

    remote(
        proj_send.at[0:TP - 1], proj_recv.at[0:TP - 1], grp_ss.at[0], grp_rs.at[0], me, tp_peer(1)
    ).wait_send()
    remote(
        frecv.at[0:ROW - 1], frecv.at[0:ROW - 1], grp_ss.at[1], grp_rs.at[1], z_peer(1), t
    ).wait_send()
    remote(
        crecv.at[0:ROW - 1], crecv.at[0:ROW - 1], grp_ss.at[2], grp_rs.at[2], z_peer(1), t
    ).wait_send()
    remote(
        srecv.at[0:PAIRS - 1], srecv.at[0:PAIRS - 1], grp_ss.at[4], grp_rs.at[4], z_peer(1), t
    ).wait_send()
    remote(
        sqrecv.at[0:TP - 1], sqrecv.at[0:TP - 1], grp_ss.at[5], grp_rs.at[5], me, tp_peer(1)
    ).wait_send()
    for kv, buf in ((0, kbuf), (1, vbuf)):
        remote(
            buf.at[0:ROW - 1], buf.at[0:ROW - 1], ring_ss.at[kv], ring_rs.at[kv, 0, 0], z_peer(1), t
        ).wait_send()
    for o in range(1, ROWS):
        @pl.when(y >= o)
        def _(o=o):
            q_copy(o).wait_send()

        @pl.when(y + o < ROWS)
        def _(o=o):
            o_copy(o).wait_send()
            y_copy(o).wait_send()
            st_copy(o).wait_send()


def per_device(
    queries, keys, values, mixer_input, gate, step_weight, state_weight, step_bias, decay_rate,
    skip_gain, norm_gain,
):
    vmem = pl.BlockSpec(memory_space=pltpu.VMEM)
    hbm = pl.BlockSpec(memory_space=pltpu.HBM)
    return pl.pallas_call(
        kernel,
        out_shape=(
            jax.ShapeDtypeStruct((TOK, 4 * HD), BF16),
            jax.ShapeDtypeStruct((TOK, 1024), BF16),
        ),
        in_specs=[hbm] * 11,
        out_specs=(vmem, vmem),
        scratch_shapes=[
            pltpu.VMEM((TOK, 4 * HD), BF16),
            pltpu.VMEM((TOK, 1024), BF16),
            pltpu.VMEM((TOK, 1024), BF16),
            pltpu.VMEM((1024, 128), BF16),
            pltpu.VMEM((32, 1024), BF16),
            pltpu.SMEM((HEADS,), F32),
            pltpu.SMEM((HEADS,), F32),
            pltpu.SMEM((HEADS,), F32),
            pltpu.VMEM((1, 1024), F32),
            pltpu.VMEM((ROW, TOK, HD), BF16),
            pltpu.VMEM((ROW, TOK, HD), BF16),
            pltpu.VMEM((3, TOK, 4 * HD), BF16),
            pltpu.VMEM((3, 4 * TOK, HD), BF16),
            pltpu.VMEM((3, 4 * TOK, HD), BF16),
            pltpu.VMEM((3, 8, TOK), F32),
            pltpu.VMEM((3, 8, TOK), F32),
            pltpu.VMEM((4, 4 * TOK, 2 * HD), F32),
            pltpu.VMEM((4, 4 * TOK, TOK), F32),
            pltpu.VMEM((TP, 48, TOK), F32),
            pltpu.VMEM((TP, 48, TOK), F32),
            pltpu.VMEM((PAIRS, STATE, TOK), BF16),
            pltpu.VMEM((ROW, STATE, TOK), BF16),
            pltpu.VMEM((PAIRS, 1, TOK), F32),
            pltpu.VMEM((ROW, 1, TOK), F32),
            pltpu.VMEM((24, TOK), F32),
            pltpu.VMEM((ROWS - 1, 24, TOK), F32),
            pltpu.VMEM((ROW, STATE, TOK), F32),
            pltpu.VMEM((PAIRS, STATE, TOK), F32),
            pltpu.VMEM((TOK, 1024), F32),
            pltpu.VMEM((TOK, 1024), F32),
            pltpu.VMEM((8, TOK), F32),
            pltpu.VMEM((TP, 8, TOK), F32),
            pltpu.VMEM((ROW, STATE, TOK), F32),
            pltpu.SemaphoreType.DMA((11,)),
            pltpu.SemaphoreType.DMA((2,)),
            pltpu.SemaphoreType.DMA((2, 2, 8)),
            pltpu.SemaphoreType.DMA((3,)),
            pltpu.SemaphoreType.DMA((3,)),
            pltpu.SemaphoreType.DMA((3,)),
            pltpu.SemaphoreType.DMA((3,)),
            pltpu.SemaphoreType.DMA((3,)),
            pltpu.SemaphoreType.DMA((3,)),
            pltpu.SemaphoreType.DMA((3,)),
            pltpu.SemaphoreType.DMA((3,)),
            pltpu.SemaphoreType.DMA((6,)),
            pltpu.SemaphoreType.DMA((6,)),
            pltpu.SemaphoreType.REGULAR((3,)),
        ],
        compiler_params=pltpu.CompilerParams(
            collective_id=0, has_side_effects=True, vmem_limit_bytes=48 << 20
        ),
    )(*[pltpu.with_memory_space_constraint(a, pltpu.HBM) for a in (
        queries, keys, values, mixer_input, gate, step_weight, state_weight.T, step_bias,
        decay_rate, skip_gain, norm_gain.reshape(1, -1),
    )])


def solution(mesh):
    return jax.shard_map(
        per_device,
        mesh=mesh,
        in_specs=(P("ctx", "tp"),) * 5 + (P("tp", None),) * 2 + (P("tp"),) * 4,
        out_specs=(P("ctx", "tp"), P("ctx", "tp")),
        check_vma=False,
    )
```

time: 56.7 us -> 52.4 us (0.924)
  Pallas kernels: 54.6 us -> 50.3 us
    pallas_call x1, Pallas kernels: 54.6 us -> 50.3 us  [per_device(): pl.pallas_call(kernel, out_shape=(jax.ShapeDtypeStruct((TOK, 4 * HD), BF1...]
where the time goes in v3:
time: 52.4 us; the launch traced here: 52.3 us
  Pallas kernels  50.3 us (96%)
  local copies, waits for them, and re-layouts  1.36 us (3%)
  between operations  0.64 us (1%)
    pallas_call x1, Pallas kernels, per_device(): pl.pallas_call(kernel, out_shape=(jax.ShapeDtypeStruct((TOK, 4 * HD), BF1...  50.3 us
    unnamed x2, local copies, waits for them, and re-layouts  1.36 us

profile of v3, /device:TPU:1, one launch (start us, length us, event | category | flops | bytes accessed | tf_op | source)
XLA Modules:
  0.0 52.3 jit_solution(1050621778798912315)
XLA Ops:
  0.6 50.3 %shard_map.122 = (bf16[128,512]{1,0:T(8,128)(2,1)S(1)}, bf16[128,1024]{1,0:T(8,128)(2,1)S(1)}) custom-call(bf16[128,512]{1,0:T(8,128)(2,1)} %q_hbm.1, bf16[128,128]{1,0:T(8,128)(2,1)} %k_hbm.1, bf16[128,128]{1,0:T(8,128)(2,1)} %v_hbm.1, bf16[128,1024]{1,0:T(8,128)(2,1)} %x_hbm.1, bf16[128,1024]{1,0:T(8,128)(2,1)} %gate_hbm.1, bf16[1024,128]{1,0:T(8,128)(2,1)} %ws_hbm.1, ...), custom_call_target="tpu_custom_call" | custom-call | tf_op jit(solution)/shard_map/pallas_call | solution.py:476
  50.9 0.7 %copy.15 = bf16[128,512]{1,0:T(8,128)(2,1)} copy(bf16[128,512]{1,0:T(8,128)(2,1)S(1)} %get-tuple-element.4) | data formatting | bytes 262144
  51.6 0.7 %copy.16 = bf16[128,1024]{1,0:T(8,128)(2,1)} copy(bf16[128,1024]{1,0:T(8,128)(2,1)S(1)} %get-tuple-element.5) | data formatting | bytes 524288

commit v4 on v3

--- a/solution.py
+++ b/solution.py
@@ -73,7 +73,7 @@
     barrier = pltpu.get_barrier_semaphore()
     for o in range(1, TP):
         signal(barrier, me, tp_peer(o))
-    for o in (1, -1):
+    for o in (1, -1, 2, -2):
         signal(barrier, z_peer(o), t)
     for o in range(1, ROWS):
         signal(barrier, y_peer(o), t)
@@ -95,40 +95,6 @@
             device_id=at(ctx, tp), device_id_type=MESH,
         )
 
-    pl.semaphore_wait(barrier, TP - 1 + 2 + ROWS - 1)
-
-    def ring_copy(kv, d, s):
-        buf = (kbuf, vbuf)[kv]
-        i = 0 if d > 0 else 1
-        src = (k_hbm, v_hbm)[kv] if s == 1 else buf.at[slot_of(-d * (s - 1))]
-        return remote(
-            src, buf.at[slot_of(-d * s)], ring_ss.at[kv], ring_rs.at[kv, i, s - 1], z_peer(d), t
-        )
-
-    def ring_steps(d):
-        return ROW // 2 if d > 0 else ROW // 2 - 1
-
-    pieces = [(kv, d) for kv in (0, 1) for d in (1, -1)]
-    for kv, d in pieces:
-        ring_copy(kv, d, 1).start()
-    for o in (1, -1):
-        signal(known.at[0], z_peer(o), t)
-
-    def ring(s):
-        for kv, d in pieces:
-            if s <= ring_steps(d):
-                ring_copy(kv, d, s).wait_recv()
-                if s + 1 <= ring_steps(d):
-                    ring_copy(kv, d, s + 1).start()
-
-    def q_copy(o):
-        return remote(q_hbm, qbuf.at[o - 1], q_ss.at[o - 1], q_rs.at[o - 1], y_peer(-o), t)
-
-    for o in range(1, ROWS):
-        @pl.when(y >= o)
-        def _(o=o):
-            q_copy(o).start()
-
     for copy in loads[:6]:
         copy.wait()
     step_part = dot(x_ref[...], ws_ref[...]).T
@@ -137,13 +103,56 @@
         proj_send[p, 0:16, :] = step_part[16 * p:16 * p + 16]
         proj_send[p, 16:48, :] = maps_part
 
+    pl.semaphore_wait(barrier, TP - 1 + 4 + ROWS - 1)
+
     def proj_copy(o):
         return remote(
             proj_send.at[tp_peer(o)], proj_recv.at[t], grp_ss.at[0], grp_rs.at[0], me, tp_peer(o)
         )
 
-    for o in range(1, TP):
+    for o in (4, 3, 5, 2, 6, 1, 7):
         proj_copy(o).start()
+
+    def ring_copy(kv, d, k):
+        buf = (kbuf, vbuf)[kv]
+        i = 0 if d > 0 else 1
+        start = (k - 1) // 2 * 2
+        src = buf.at[slot_of(-d * start)] if start else (k_hbm, v_hbm)[kv]
+        return remote(
+            src, buf.at[slot_of(-d * k)], ring_ss.at[kv], ring_rs.at[kv, i, k - 1],
+            z_peer(d * (k - start)), t,
+        )
+
+    def reach(d):
+        return ROW // 2 if d > 0 else ROW // 2 - 1
+
+    pieces = [(kv, d) for kv in (0, 1) for d in (1, -1)]
+
+    def ring_send(kv, d, start):
+        for k in (start + 2, start + 1):
+            if k <= reach(d):
+                ring_copy(kv, d, k).start()
+
+    for kv, d in pieces:
+        ring_send(kv, d, 0)
+    for o in (2, -2):
+        signal(known.at[0], z_peer(o), t)
+
+    def ring(stage):
+        for kv, d in pieces:
+            if 2 * stage <= reach(d):
+                ring_copy(kv, d, 2 * stage).wait_recv()
+                ring_send(kv, d, 2 * stage)
+        for kv, d in pieces:
+            ring_copy(kv, d, 2 * stage - 1).wait_recv()
+
+    def q_copy(o):
+        return remote(q_hbm, qbuf.at[o - 1], q_ss.at[o - 1], q_rs.at[o - 1], y_peer(-o), t)
+
+    for o in range(1, ROWS):
+        @pl.when(y >= o)
+        def _(o=o):
+            q_copy(o).start()
 
     lane = lax.broadcasted_iota(jnp.int32, (TOK, TOK), 1)
     sub = lax.broadcasted_iota(jnp.int32, (TOK, TOK), 0)
@@ -158,20 +167,14 @@
         return out
 
     bias, rate = column(bias_ref), column(rate_ref)
-    pl.semaphore_wait(known.at[0], 2)
-    for o in (2, -2):
-        signal(known.at[1], z_peer(o), t)
-
 
     def greet_far():
-        pl.semaphore_wait(known.at[1], 2)
+        pl.semaphore_wait(known.at[0], 2)
         for o in (4, -4):
-            signal(known.at[2], z_peer(o), t)
+            signal(known.at[1], z_peer(o), t)
 
     pl.when(z >= 6)(greet_far)
     ring(1)
-    ring(2)
-
     remote(
         proj_send.at[0:TP - 1], proj_recv.at[0:TP - 1], grp_ss.at[0], grp_rs.at[0], me, tp_peer(1)
     ).wait_recv()
@@ -202,7 +205,7 @@
         csend[j] = dot(feed, pair_input(j)).astype(BF16)
 
     pl.when(z < 6)(greet_far)
-    pl.semaphore_wait(known.at[2], 2)
+    pl.semaphore_wait(known.at[1], 2)
 
     def f_copy(o):
         return remote(
@@ -220,7 +223,6 @@
         c_copy(o).start()
     crecv[z] = csend[lax.rem(z, PAIRS)]
     frecv[z] = fsend[lax.rem(z, PAIRS)]
-    ring(3)
     turned = jnp.concatenate([c_rows, climb, jnp.exp(climb), jnp.zeros((80, TOK), F32)], axis=0).T
     c_cols = turned[:, 0:16]
     inner = dot(c_cols, b_rows, EXACT)
@@ -301,8 +303,8 @@
     for copy in loads[6:]:
         copy.wait()
     attend_some(0, 1, 2, 3, 0)
-    ring(4)
-    attend_some(1, 1, 2)
+    ring(2)
+    attend_some(1, 1, 2, 3, 0)
     remote(
         frecv.at[0:ROW - 1], frecv.at[0:ROW - 1], grp_ss.at[1], grp_rs.at[1], z_peer(1), t
     ).wait_recv()
@@ -328,9 +330,7 @@
         def _(o=o):
             y_copy(o).start()
 
-    ring(5)
-
-    attend_some(1, 3, 0)
+    ring(3)
     for o in range(1, ROWS):
         @pl.when(y >= o)
         def _(o=o):
@@ -355,12 +355,8 @@
     for o in (-4, 3, -3, 2, -2, 1, -1):
         r_copy(o).start()
     srecv[lax.rem(z, PAIRS)] = rsend[z]
-    ring(6)
-    attend_some(2, 3, 2)
-    ring(7)
-    attend_some(2, 1, 0)
-    ring(8)
-
+    attend_some(2, 1, 2, 3, 0)
+    ring(4)
     def o_copy(o):
         return remote(
             obuf.at[o - 1], orecv.at[o - 1], o_ss.at[o - 1], o_rs.at[o - 1], y_peer(o), t
@@ -528,7 +524,7 @@
             pltpu.SemaphoreType.DMA((3,)),
             pltpu.SemaphoreType.DMA((6,)),
             pltpu.SemaphoreType.DMA((6,)),
-            pltpu.SemaphoreType.REGULAR((3,)),
+            pltpu.SemaphoreType.REGULAR((2,)),
         ],
         compiler_params=pltpu.CompilerParams(
             collective_id=0, has_side_effects=True, vmem_limit_bytes=48 << 20

time: 52.4 us -> 47.7 us (0.910)
  Pallas kernels: 50.3 us -> 45.6 us
    pallas_call x1, Pallas kernels: 50.3 us -> 45.6 us  [per_device(): pl.pallas_call(kernel, out_shape=(jax.ShapeDtypeStruct((TOK, 4 * HD), BF1...]
where the time goes in v4:
time: 47.7 us; the launch traced here: 47.6 us
  Pallas kernels  45.6 us (96%)
  local copies, waits for them, and re-layouts  1.36 us (3%)
  between operations  0.64 us (1%)
    pallas_call x1, Pallas kernels, per_device(): pl.pallas_call(kernel, out_shape=(jax.ShapeDtypeStruct((TOK, 4 * HD), BF1...  45.6 us
    unnamed x2, local copies, waits for them, and re-layouts  1.36 us

profile of v4, /device:TPU:1, one launch (start us, length us, event | category | flops | bytes accessed | tf_op | source)
XLA Modules:
  0.0 47.6 jit_solution(17781022665528266152)
XLA Ops:
  0.6 45.6 %shard_map.122 = (bf16[128,512]{1,0:T(8,128)(2,1)S(1)}, bf16[128,1024]{1,0:T(8,128)(2,1)S(1)}) custom-call(bf16[128,512]{1,0:T(8,128)(2,1)} %q_hbm.1, bf16[128,128]{1,0:T(8,128)(2,1)} %k_hbm.1, bf16[128,128]{1,0:T(8,128)(2,1)} %v_hbm.1, bf16[128,1024]{1,0:T(8,128)(2,1)} %x_hbm.1, bf16[128,1024]{1,0:T(8,128)(2,1)} %gate_hbm.1, bf16[1024,128]{1,0:T(8,128)(2,1)} %ws_hbm.1, ...), custom_call_target="tpu_custom_call" | custom-call | tf_op jit(solution)/shard_map/pallas_call | solution.py:472
  46.2 0.7 %copy.15 = bf16[128,512]{1,0:T(8,128)(2,1)} copy(bf16[128,512]{1,0:T(8,128)(2,1)S(1)} %get-tuple-element.4) | data formatting | bytes 262144
  46.9 0.7 %copy.16 = bf16[128,1024]{1,0:T(8,128)(2,1)} copy(bf16[128,1024]{1,0:T(8,128)(2,1)S(1)} %get-tuple-element.5) | data formatting | bytes 524288

commit v5 on v4

--- a/solution.py
+++ b/solution.py
@@ -128,13 +128,13 @@
 
     pieces = [(kv, d) for kv in (0, 1) for d in (1, -1)]
 
-    def ring_send(kv, d, start):
-        for k in (start + 2, start + 1):
-            if k <= reach(d):
-                ring_copy(kv, d, k).start()
-
-    for kv, d in pieces:
-        ring_send(kv, d, 0)
+    def ring_send(kv, d, k):
+        if k <= reach(d):
+            ring_copy(kv, d, k).start()
+
+    for k in (2, 1):
+        for kv, d in pieces:
+            ring_send(kv, d, k)
     for o in (2, -2):
         signal(known.at[0], z_peer(o), t)
 
@@ -142,7 +142,9 @@
         for kv, d in pieces:
             if 2 * stage <= reach(d):
                 ring_copy(kv, d, 2 * stage).wait_recv()
-                ring_send(kv, d, 2 * stage)
+                ring_send(kv, d, 2 * stage + 2)
+        for kv, d in pieces:
+            ring_send(kv, d, 2 * stage + 1)
         for kv, d in pieces:
             ring_copy(kv, d, 2 * stage - 1).wait_recv()
 
@@ -463,18 +465,30 @@
             st_copy(o).wait_send()
 
 
+def write_out(attn, mamba, attn_hbm, mamba_hbm, sems):
+    copies = [
+        pltpu.make_async_copy(attn, attn_hbm, sems.at[0]),
+        pltpu.make_async_copy(mamba, mamba_hbm, sems.at[1]),
+    ]
+    for copy in copies:
+        copy.start()
+    for copy in copies:
+        copy.wait()
+
+
 def per_device(
     queries, keys, values, mixer_input, gate, step_weight, state_weight, step_bias, decay_rate,
     skip_gain, norm_gain,
 ):
     vmem = pl.BlockSpec(memory_space=pltpu.VMEM)
     hbm = pl.BlockSpec(memory_space=pltpu.HBM)
-    return pl.pallas_call(
+    shapes = (
+        jax.ShapeDtypeStruct((TOK, 4 * HD), BF16),
+        jax.ShapeDtypeStruct((TOK, 1024), BF16),
+    )
+    results = pl.pallas_call(
         kernel,
-        out_shape=(
-            jax.ShapeDtypeStruct((TOK, 4 * HD), BF16),
-            jax.ShapeDtypeStruct((TOK, 1024), BF16),
-        ),
+        out_shape=shapes,
         in_specs=[hbm] * 11,
         out_specs=(vmem, vmem),
         scratch_shapes=[
@@ -534,6 +548,15 @@
         decay_rate, skip_gain, norm_gain.reshape(1, -1),
     )])
 
+    return pl.pallas_call(
+        write_out,
+        out_shape=shapes,
+        in_specs=[pl.BlockSpec(memory_space=pltpu.VMEM)] * 2,
+        out_specs=(hbm, hbm),
+        scratch_shapes=[pltpu.SemaphoreType.DMA((2,))],
+        compiler_params=pltpu.CompilerParams(vmem_limit_bytes=8 << 20),
+    )(*results)
+
 
 def solution(mesh):
     return jax.shard_map(

time: 47.7 us -> 46.2 us (0.969)
  local copies, waits for them, and re-layouts: 1.36 us -> 0 us
    unnamed x2 -> x0, local copies, waits for them, and re-layouts: 1.36 us -> none
    pallas_call x1 -> x2, Pallas kernels: 45.6 us -> 45.3 us  [the longest x1 44.5 us: per_device(): pl.pallas_call(kernel, out_shape=shapes, in_specs=[hbm] * 11, out_specs=(...]
where the time goes in v5:
time: 46.2 us; the launch traced here: 46.1 us
  Pallas kernels  45.3 us (98%)
  between operations  0.8 us (2%)
    pallas_call x1, Pallas kernels, per_device(): pl.pallas_call(kernel, out_shape=shapes, in_specs=[hbm] * 11, out_specs=(...  44.5 us

profile of v5, /device:TPU:1, one launch (start us, length us, event | category | flops | bytes accessed | tf_op | source)
XLA Modules:
  0.0 46.1 jit_solution(6743771869182734451)
XLA Ops:
  0.6 44.5 %shard_map.122 = (bf16[128,512]{1,0:T(8,128)(2,1)S(1)}, bf16[128,1024]{1,0:T(8,128)(2,1)S(1)}) custom-call(bf16[128,512]{1,0:T(8,128)(2,1)} %q_hbm.1, bf16[128,128]{1,0:T(8,128)(2,1)} %k_hbm.1, bf16[128,128]{1,0:T(8,128)(2,1)} %v_hbm.1, bf16[128,1024]{1,0:T(8,128)(2,1)} %x_hbm.1, bf16[128,1024]{1,0:T(8,128)(2,1)} %gate_hbm.1, bf16[1024,128]{1,0:T(8,128)(2,1)} %ws_hbm.1, ...), custom_call_target="tpu_custom_call" | custom-call | tf_op jit(solution)/shard_map/pallas_call | solution.py:489
  45.1 0.8 %shard_map.123 = (bf16[128,512]{1,0:T(8,128)(2,1)}, bf16[128,1024]{1,0:T(8,128)(2,1)}) custom-call(bf16[128,512]{1,0:T(8,128)(2,1)S(1)} %get-tuple-element.4.attn, bf16[128,1024]{1,0:T(8,128)(2,1)S(1)} %get-tuple-element.5.mamba), custom_call_target="tpu_custom_call" | custom-call | tf_op jit(solution)/shard_map/pallas_call | solution.py:551
